TPU v7x, 128 devices: a whole 4x4x4 slice. The times are simulated.
128 devices in a mesh: occ: 16 (over x_lo, z, core), aux: 8 (over y, x_hi).
Axes of the slice: x: 4 (x_hi: 2, x_lo: 2; x = x_hi * 2 + x_lo), y: 4, z: 4, core: 2. Of those that a mesh axis runs over, the one named last changes fastest.
Arguments:
- integrals: bfloat16 [2048, 256, 512], P('aux', 'occ'), may hold values from -1.1953125 to 1.1953125
- metric: bfloat16 [2048, 2048], replicated, may hold values from -0.125 to 0.125
- e_occ: float32 [256], replicated, may hold values from -2 to -0.3
- e_vir: float32 [512], replicated, may hold values from 0.2 to 3
- partner: int32 [256, 2], P(('occ', 'aux')), may hold values from 0 to 1
- screen: int32 [256, 2], P(('occ', 'aux')), may hold values from 0 to 1
Outputs:
- gradient: bfloat16 [2048, 256, 512], P(None, ('occ', 'aux'))
- density: float32 [512, 512], P('occ')
All inputs are finite; a program needn't handle non-finite values.
Results may differ from a plain program's by a relative error of at most 0.0055.
Values may be sent and summed in bfloat16 or wider, within the bound.
No kernel may reach another device: no remote copies, remote signals or barrier semaphores. Data moves between devices by JAX's collectives and lax.ppermute only.
A program may use at most 128 MiB of HBM per device.

v0:
```python
import jax
import jax.numpy as jnp
from jax import lax
from jax.sharding import PartitionSpec as P

NOCC = 256
ROUNDS = 2


def passed_along(array, axis, by):
    count = lax.axis_size(axis)
    return lax.ppermute(array, axis, [(i, (i + by) % count) for i in range(count)])


def split_up(array, dim, count):
    before, after = (array.shape[:dim], array.shape[dim + 1 :])
    return jnp.moveaxis(array.reshape(*before, count, -1, *after), dim, 0)


def sum_at_owner(array, axis, dim):
    pieces = split_up(array, dim, lax.axis_size(axis))
    arrived = lax.all_to_all(pieces, axis, split_axis=0, concat_axis=0, tiled=True)
    return arrived.astype(jnp.float32).sum(axis=0)


def from_everyone(array, axis):
    count = lax.axis_size(axis)
    return lax.all_to_all(
        jnp.broadcast_to(array[None], (count, *array.shape)), axis, 0, 0, tiled=True
    )


def of_everyone(array, axis):
    return from_everyone(array, axis).astype(jnp.float32).sum(axis=0)


def transform(metric, moved):
    shape = moved.shape
    mixed = jnp.dot(metric, moved.reshape(shape[0], -1), preferred_element_type=jnp.float32)
    return mixed.astype(jnp.bfloat16).reshape(shape)


def fetch_block(coeff, offset):
    return passed_along(coeff, ("occ", "aux"), offset)


def on_device(integrals, metric, e_occ, e_vir, partner, screen):
    groups = lax.axis_size(("occ", "aux"))
    moved = lax.all_to_all(integrals, "aux", split_axis=1, concat_axis=0, tiled=True)
    coeff = transform(metric, moved)
    naux, own, nvir = coeff.shape
    device = lax.axis_index(("occ", "aux"))
    pair_sum = e_vir[:, None] + e_vir[None, :]
    gamma = jnp.zeros((naux, own, nvir), jnp.float32)
    density = jnp.zeros((nvir, nvir), jnp.float32)
    shifts = (1, groups // 2)
    for rnd in range(ROUNDS):
        offset = shifts[rnd % 2]
        fetched = fetch_block(coeff, offset)
        source = (device - offset) % groups

        def one_pair(carry, slot, rnd=rnd, fetched=fetched, source=source):
            grad_acc, dens_acc = carry
            local = partner[slot, rnd]
            kept = screen[slot, rnd].astype(jnp.float32)
            left = lax.dynamic_index_in_dim(coeff, slot, 1, False)
            right = lax.dynamic_index_in_dim(fetched, local, 1, False)
            intersection = lax.dot_general(
                left, right, (((0,), (0,)), ((), ())), preferred_element_type=jnp.float32
            )
            gap = pair_sum - e_occ[device * own + slot] - e_occ[source * own + local]
            amp = (kept * intersection / gap).astype(jnp.bfloat16)
            term = lax.dot_general(
                right, amp, (((1,), (1,)), ((), ())), preferred_element_type=jnp.float32
            )
            column = lax.dynamic_index_in_dim(grad_acc, slot, 1, False) + term
            grad_acc = lax.dynamic_update_index_in_dim(grad_acc, column, slot, 1)
            dens_acc = dens_acc + lax.dot_general(
                amp, amp, (((1,), (1,)), ((), ())), preferred_element_type=jnp.float32
            )
            return (grad_acc, dens_acc)

        def visit(slot, carry, rnd=rnd, one_pair=one_pair):
            return one_pair(carry, slot)

        gamma, density = lax.fori_loop(0, own, visit, (gamma, density))
    rows = sum_at_owner(density.astype(jnp.bfloat16), "occ", 0)
    block = of_everyone(rows.astype(jnp.bfloat16), "aux").astype(jnp.float32)
    return (gamma.astype(jnp.bfloat16), block / NOCC)


def solution(mesh):
    placed = (
        P("aux", "occ", None),
        P(),
        P(),
        P(),
        P(("occ", "aux"), None),
        P(("occ", "aux"), None),
    )
    return jax.shard_map(
        on_device,
        mesh=mesh,
        in_specs=placed,
        out_specs=(P(None, ("occ", "aux"), None), P("occ", None)),
        check_vma=False,
    )
```

profile of v0, /device:TPU:4, one launch (start us, length us, event | category | flops | bytes accessed | tf_op | source)
XLA Modules:
  0.0 348.9 jit_solution(17840676063706415823)
XLA Ops:
  0.6 4.5 %copy.26 = bf16[256,16,512]{2,0,1:T(8,128)(2,1)S(1)} copy(bf16[256,16,512]{2,1,0:T(8,128)(2,1)} %param.10) | data formatting | bytes 8388608 | tf_op args[0]
  5.2 55.9 %all_to_all.25 = bf16[256,16,512]{2,0,1:T(8,128)(2,1)} all-to-all(bf16[256,16,512]{2,0,1:T(8,128)(2,1)S(1)} %copy.26), channel_id=1, replica_groups=mesh['occ'=16,'aux'=8] {'aux'}, dimensions={1} | all-to-all | bytes 8388608 | tf_op jit(solution)/shard_map/all_to_all | solution.py:49
  61.0 8.0 %copy.27 = bf16[256,8,2,512]{0,1,3,2:T(8,128)(2,1)} copy(bf16[256,8,2,512]{3,0,2,1:T(8,128)(2,1)} %bitcast.109) | data formatting | bytes 8388608 | tf_op jit(solution)/shard_map/all_to_all | solution.py:49
  69.0 3.7 %copy.33 = bf16[128,8,8,256]{3,1,2,0:T(8,128)(2,1)S(1)} copy(bf16[128,8,8,256]{3,2,1,0:T(8,128)(2,1)} %bitcast.110) | data formatting | bytes 8388608
  72.7 12.6 %convolution_convert_fusion = bf16[2048,1024]{0,1:T(8,128)(2,1)} fusion(bf16[2048,2048]{1,0:T(8,128)(2,1)} %param.11, bf16[2048,1024]{0,1:T(8,128)(2,1)S(1)} %bitcast.111), kind=kOutput, calls=%fused_computation.41 | convolution fusion | flops 8592031744 | bytes 16777216 | tf_op jit(solution)/shard_map/dot_general | solution.py:39
  85.3 6.3 %copy.28 = bf16[2048,2,512]{2,0,1:T(8,128)(2,1)} copy(bf16[2048,2,512]{0,2,1:T(8,128)(2,1)} %bitcast.112) | data formatting | bytes 8388608 | tf_op jit(solution)/shard_map/reshape | solution.py:40
  91.6 2.1 collective-permute-start
  93.6 1.7 collective-permute-start.1
  95.4 91.5 %collective-permute-done = bf16[2048,2,512]{2,0,1:T(8,128)(2,1)} collective-permute-done((bf16[2048,2,512]{2,0,1:T(8,128)(2,1)}, bf16[2048,2,512]{2,0,1:T(8,128)(2,1)}, u32[]{:S(2)}, u32[]{:S(2)}) %collective-permute-start) | collective-permute-done | bytes 4194336 | tf_op jit(solution)/shard_map/ppermute | solution.py:12
  186.9 4.3 %broadcast_in_dim.33 = f32[2048,2,512]{2,0,1:T(8,128)} broadcast(f32[]{:T(128)} %constant.139.clone.1), dimensions={} | broadcast | bytes 8388612 | tf_op jit(solution)/shard_map/broadcast_in_dim | solution.py:54
  191.2 35.1 %while.37 = (s32[]{:T(128)}, f32[2048,2,512]{2,0,1:T(8,128)}, f32[512,512]{1,0:T(8,128)S(1)}, s32[2,2]{1,0:T(2,128)S(1)}, bf16[2048,2,512]{2,0,1:T(8,128)(2,1)},...) while((s32[]{:T(128)}, f32[2048,2,512]{2,0,1:T(8,128)}, ...), condition=%wide.region_1.2_spmd.clone, body=%wide.region_0.1_spmd.clone.sunk | while | flops 2419064832 | bytes 26745676 | solution.py:86
  192.5 0.7 fusion.78
  195.3 5.4 %fusion.79 = bf16[512,512]{1,0:T(8,128)(2,1)S(1)} fusion(bf16[2048,2,512]{2,0,1:T(8,128)(2,1)} %get-tuple-element.908, s32[]{:T(128)S(6)} %select_n.108, bf16[2048,2,512]{2,0,1:T(8,128)(2,1)} %get-tuple-element.910, s32[]{:T(128)} %get-tuple-element.889, f32[512]{0:T(512)S(1)} %get-tuple-element.914, f32[]{:T(128)} %bitcast.106, f32[]{:T(128)} %bitcast.107, ...), kind=kOutput, calls=%fused_computation.34.clone.1 | convolution fusion | flops 1075314688 | bytes 4724740 | tf_op jit(solution)/shard_map/while/body/eval_jaxpr/dot_general | solution.py:68
  200.7 2.6 constant_dynamic-slice_fusion.12
  203.3 4.8 %bitcast_dynamic-update-slice_fusion.5 = f32[2048,2,512]{2,0,1:T(8,128)} fusion(f32[2048,2,512]{2,0,1:T(8,128)} %get-tuple-element.890, s32[]{:T(128)} %get-tuple-element.889, f32[2048,1,512]{2,0,1:T(8,128)S(1)} %constant_dynamic-slice_fusion.12, bf16[512,512]{1,0:T(8,128)(2,1)S(1)} %fusion.79, bf16[2048,2,512]{2,0,1:T(8,128)(2,1)} %get-tuple-element.908, ...), kind=kOutput, calls=%fused_computation.21.clone.1 | convolution fusion | flops 1074790400 | bytes 11010564 | tf_op jit(solution)/shard_map/while/body/eval_jaxpr/dot_general | solution.py:73
  210.1 0.7 fusion.78
  212.8 5.4 %fusion.79 = bf16[512,512]{1,0:T(8,128)(2,1)S(1)} fusion(bf16[2048,2,512]{2,0,1:T(8,128)(2,1)} %get-tuple-element.908, s32[]{:T(128)S(6)} %select_n.108, bf16[2048,2,512]{2,0,1:T(8,128)(2,1)} %get-tuple-element.910, s32[]{:T(128)} %get-tuple-element.889, f32[512]{0:T(512)S(1)} %get-tuple-element.914, f32[]{:T(128)} %bitcast.106, f32[]{:T(128)} %bitcast.107, ...), kind=kOutput, calls=%fused_computation.34.clone.1 | convolution fusion | flops 1075314688 | bytes 4724740 | tf_op jit(solution)/shard_map/while/body/eval_jaxpr/dot_general | solution.py:68
  218.2 2.6 constant_dynamic-slice_fusion.12
  220.8 4.9 %bitcast_dynamic-update-slice_fusion.5 = f32[2048,2,512]{2,0,1:T(8,128)} fusion(f32[2048,2,512]{2,0,1:T(8,128)} %get-tuple-element.890, s32[]{:T(128)} %get-tuple-element.889, f32[2048,1,512]{2,0,1:T(8,128)S(1)} %constant_dynamic-slice_fusion.12, bf16[512,512]{1,0:T(8,128)(2,1)S(1)} %fusion.79, bf16[2048,2,512]{2,0,1:T(8,128)(2,1)} %get-tuple-element.908, ...), kind=kOutput, calls=%fused_computation.21.clone.1 | convolution fusion | flops 1074790400 | bytes 11010564 | tf_op jit(solution)/shard_map/while/body/eval_jaxpr/dot_general | solution.py:73
  226.3 47.6 %collective-permute-done.1 = bf16[2048,2,512]{2,0,1:T(8,128)(2,1)} collective-permute-done((bf16[2048,2,512]{2,0,1:T(8,128)(2,1)}, bf16[2048,2,512]{2,0,1:T(8,128)(2,1)}, u32[]{:S(2)}, u32[]{:S(2)}) %collective-permute-start.1) | collective-permute-done | bytes 4194336 | tf_op jit(solution)/shard_map/ppermute | solution.py:12
  273.9 34.3 %while.36 = (s32[]{:T(128)}, f32[2048,2,512]{2,0,1:T(8,128)}, f32[512,512]{1,0:T(8,128)S(1)}, s32[2,2]{1,0:T(2,128)S(1)}, bf16[2048,2,512]{2,0,1:T(8,128)(2,1)},...) while((s32[]{:T(128)}, f32[2048,2,512]{2,0,1:T(8,128)}, ...), condition=%wide.region_3.4_spmd.clone, body=%wide.region_2.3_spmd.clone.sunk | while | flops 2418802688 | bytes 26745668 | solution.py:86
  275.1 0.6 fusion.70
  277.7 5.3 %fusion.71 = bf16[512,512]{1,0:T(8,128)(2,1)S(1)} fusion(bf16[2048,2,512]{2,0,1:T(8,128)(2,1)} %get-tuple-element.953, s32[]{:T(128)S(6)} %select_n.105, bf16[2048,2,512]{2,0,1:T(8,128)(2,1)} %get-tuple-element.955, s32[]{:T(128)} %get-tuple-element.934, f32[512]{0:T(512)S(1)} %get-tuple-element.959, f32[]{:T(128)} %bitcast.94, f32[]{:T(128)} %bitcast.95, ...), kind=kOutput, calls=%fused_computation.15.clone.1 | convolution fusion | flops 1075314688 | bytes 4724740 | tf_op jit(solution)/shard_map/while/body/eval_jaxpr/dot_general | solution.py:68
  283.0 2.6 constant_dynamic-slice_fusion.10
  285.7 4.8 %bitcast_dynamic-update-slice_fusion.4 = f32[2048,2,512]{2,0,1:T(8,128)} fusion(f32[2048,2,512]{2,0,1:T(8,128)} %get-tuple-element.935, s32[]{:T(128)} %get-tuple-element.934, f32[2048,1,512]{2,0,1:T(8,128)S(1)} %constant_dynamic-slice_fusion.10, bf16[512,512]{1,0:T(8,128)(2,1)S(1)} %fusion.71, bf16[2048,2,512]{2,0,1:T(8,128)(2,1)} %get-tuple-element.953, ...), kind=kOutput, calls=%fused_computation.2.clone.1 | convolution fusion | flops 1074790400 | bytes 11010564 | tf_op jit(solution)/shard_map/while/body/eval_jaxpr/dot_general | solution.py:73
  294.9 5.3 %fusion.71 = bf16[512,512]{1,0:T(8,128)(2,1)S(1)} fusion(bf16[2048,2,512]{2,0,1:T(8,128)(2,1)} %get-tuple-element.953, s32[]{:T(128)S(6)} %select_n.105, bf16[2048,2,512]{2,0,1:T(8,128)(2,1)} %get-tuple-element.955, s32[]{:T(128)} %get-tuple-element.934, f32[512]{0:T(512)S(1)} %get-tuple-element.959, f32[]{:T(128)} %bitcast.94, f32[]{:T(128)} %bitcast.95, ...), kind=kOutput, calls=%fused_computation.15.clone.1 | convolution fusion | flops 1075314688 | bytes 4724740 | tf_op jit(solution)/shard_map/while/body/eval_jaxpr/dot_general | solution.py:68
  300.2 2.6 constant_dynamic-slice_fusion.10
  302.8 4.9 %bitcast_dynamic-update-slice_fusion.4 = f32[2048,2,512]{2,0,1:T(8,128)} fusion(f32[2048,2,512]{2,0,1:T(8,128)} %get-tuple-element.935, s32[]{:T(128)} %get-tuple-element.934, f32[2048,1,512]{2,0,1:T(8,128)S(1)} %constant_dynamic-slice_fusion.10, bf16[512,512]{1,0:T(8,128)(2,1)S(1)} %fusion.71, bf16[2048,2,512]{2,0,1:T(8,128)(2,1)} %get-tuple-element.953, ...), kind=kOutput, calls=%fused_computation.2.clone.1 | convolution fusion | flops 1074790400 | bytes 11010564 | tf_op jit(solution)/shard_map/while/body/eval_jaxpr/dot_general | solution.py:73
  308.3 16.2 %all_to_all.26 = bf16[16,32,512]{2,1,0:T(8,128)(2,1)S(1)} all-to-all(bf16[16,32,512]{2,1,0:T(8,128)(2,1)S(1)} %bitcast.113), channel_id=1, replica_groups=mesh['occ'=16,'aux'=8] {'occ'}, dimensions={0} | all-to-all | bytes 1048576 | tf_op jit(solution)/shard_map/all_to_all | solution.py:22
  324.5 0.7 broadcast_in_dim.35
  325.3 7.8 %all-to-all-start.2 = ((bf16[8,32,512]{2,1,0:T(8,128)(2,1)}), bf16[8,32,512]{2,1,0:T(8,128)(2,1)S(1)}, u32[]{:S(2)}, u32[]{:S(2)}) async-start(bf16[8,32,512]{2,1,0:T(8,128)(2,1)} %broadcast_in_dim.35), calls=%async_computation.2 | async-start | bytes 524288 | tf_op jit(solution)/shard_map/all_to_all | solution.py:28
  333.0 15.2 %copy.35 = bf16[2048,2,512]{2,1,0:T(2,128)(2,1)} copy(f32[2048,2,512]{2,0,1:T(8,128)} %get-tuple-element.518) | data formatting | bytes 12582912 | tf_op jit(solution)/shard_map/while | solution.py:86
  (23 shorter events, 6.0 us)
Async XLA Ops:
  91.6 95.3 %collective-permute-start = (bf16[2048,2,512]{2,0,1:T(8,128)(2,1)}, bf16[2048,2,512]{2,0,1:T(8,128)(2,1)}, u32[]{:S(2)}, u32[]{:S(2)}) collective-permute-start(bf16[2048,2,512]{2,0,1:T(8,128)(2,1)} %copy.28), channel_id=1, source_target_pairs={{0,1},{1,2},{2,3},{3,4},{4,5},{5,6},{6,7},{7,8},{8,9},{9,10},{10,1... | collective-permute-start | bytes 12582920 | tf_op jit(solution)/shard_map/ppermute | solution.py:12
  93.6 180.3 %collective-permute-start.1 = (bf16[2048,2,512]{2,0,1:T(8,128)(2,1)}, bf16[2048,2,512]{2,0,1:T(8,128)(2,1)}, u32[]{:S(2)}, u32[]{:S(2)}) collective-permute-start(bf16[2048,2,512]{2,0,1:T(8,128)(2,1)} %copy.28), channel_id=1, source_target_pairs={{0,64},{1,65},{2,66},{3,67},{4,68},{5,69},{6,70},{7,71},{8,72},{9,... | collective-permute-start | bytes 12582920 | tf_op jit(solution)/shard_map/ppermute | solution.py:12
  95.3 95.9 %copy-start = (f32[256]{0:T(256)S(1)}, f32[256]{0:T(256)}, u32[]{:S(2)}) copy-start(f32[256]{0:T(256)} %param.12) | copy-start | bytes 3076
  95.3 95.9 %copy-start.1 = (s32[2,2]{1,0:T(2,128)S(1)}, s32[2,2]{1,0:T(2,128)}, u32[]{:S(2)}) copy-start(s32[2,2]{1,0:T(2,128)} %param.14) | copy-start | bytes 52
  95.3 95.9 %copy-start.2 = (s32[2,2]{1,0:T(2,128)S(1)}, s32[2,2]{1,0:T(2,128)}, u32[]{:S(2)}) copy-start(s32[2,2]{1,0:T(2,128)} %param.15) | copy-start | bytes 52
  95.3 95.9 %copy-start.3 = (f32[512]{0:T(512)S(1)}, f32[512]{0:T(512)}, u32[]{:S(2)}) copy-start(f32[512]{0:T(512)} %param.13) | copy-start | bytes 6148
  325.3 22.9 %all-to-all-start.2 = ((bf16[8,32,512]{2,1,0:T(8,128)(2,1)}), bf16[8,32,512]{2,1,0:T(8,128)(2,1)S(1)}, u32[]{:S(2)}, u32[]{:S(2)}) async-start(bf16[8,32,512]{2,1,0:T(8,128)(2,1)} %broadcast_in_dim.35), calls=%async_computation.2 | async-start | bytes 524288 | tf_op jit(solution)/shard_map/all_to_all | solution.py:28
where the time goes:
time: 350 us; the launch traced here: 349 us
  waiting for transfers between devices  139 us (40%)
  blocking collectives  72.1 us (21%)
  local copies, waits for them, and re-layouts  55.9 us (16%)
  matrix products  55.5 us (16%)
  starting transfers between devices  11.5 us (3%)
  loops' own time  10.9 us (3%)
    ppermute x2, waiting for transfers between devices, passed_along(): lax.ppermute(array, axis, [(i, (i + by) % count) for i in range(count)])  139 us
    all_to_all x1, blocking collectives, on_device(): lax.all_to_all(integrals, 'aux', split_axis=1, concat_axis=0, tiled=True)  55.9 us
    dot_general x4, matrix products, one_pair(): lax.dot_general(left, right, (((0,), (0,)), ((), ())), preferred_element_...  21.4 us
    dot_general x4, matrix products, one_pair(): lax.dot_general(right, amp, (((1,), (1,)), ((), ())), preferred_element_t...  19.4 us
    all_to_all x1, blocking collectives, sum_at_owner(): lax.all_to_all(pieces, axis, split_axis=0, concat_axis=0, tiled=True)  16.2 us
    while x1, local copies, waits for them, and re-layouts, on_device(): gamma, density = lax.fori_loop(0, own, visit, (gamma, density))  15.2 us
    dot_general x1, matrix products, transform(): jnp.dot(metric, moved.reshape(shape[0], -1), preferred_element_type=jnp.f...  12.6 us
    another operation x2, loops' own time, on_device(): gamma, density = lax.fori_loop(0, own, visit, (gamma, density))  10.9 us
  transfers between devices with their start and end apart: 3, of which 2 were waited for; matrix products, arithmetic and copies ran while one was open for 14% of the time, Pallas kernels for 0%

commit v1 on v0

v1 whole, which is shorter than its diff:
```python
import jax
import jax.numpy as jnp
from jax import lax
from jax.experimental import pallas as pl
from jax.experimental.pallas import tpu as pltpu
from jax.sharding import PartitionSpec as P

NOCC = 256
AXES = ("occ", "aux")
ROWS = 256
VMEM = 60 * 1024 * 1024


def along_y(by):
    return lambda l: (l & ~6) | (((((l >> 1) & 3) + by) % 4) << 1)


def same_hop(l):
    return l ^ 64


def other_hop(l):
    return l ^ 65


def onward_hop(l):
    to = l ^ 65
    return to if to & 1 else (to + 2) % 128


def before_hop(by):
    def to(l):
        y = (((l >> 1) & 3) + by) % 4
        there = (l & ~6) | (y << 1)
        return (there + 8) % 128 if y == 0 else there

    return to


def send(array, to, after=(), only=lambda l: True):
    if after:
        array = lax.optimization_barrier((array, *after))[0]
    return lax.ppermute(array, AXES, [(l, to(l)) for l in range(128) if only(l)])


def transform_kernel(count, ids, *refs):
    metric = jnp.concatenate([ref[...] for ref in refs[:count]], axis=1)
    out = refs[-1]
    for slot in range(2):
        right = jnp.concatenate([ref[slot] for ref in refs[count : 2 * count]], axis=0)
        mixed = jnp.dot(metric, right, preferred_element_type=jnp.float32)
        out[slot] = mixed.astype(out.dtype)


def transform(metric, ids, pieces, tile=512):
    count = len(pieces)
    naux = metric.shape[0]
    nvir = pieces[0][0].shape[-1]
    columns = [
        pl.BlockSpec((tile, ROWS), lambda m, ids, k=k: (m, ids[k])) for k in range(count)
    ]
    rows = [
        pl.BlockSpec((None, 2, ROWS, nvir), lambda m, ids, n=n: (n, 0, 0, 0)) for _, n in pieces
    ]
    flops = 2 * naux * count * ROWS * 2 * nvir
    return pl.pallas_call(
        lambda *refs: transform_kernel(count, *refs),
        out_shape=jax.ShapeDtypeStruct((2, naux, nvir), jnp.bfloat16),
        grid_spec=pltpu.PrefetchScalarGridSpec(
            num_scalar_prefetch=1,
            grid=(naux // tile,),
            in_specs=columns + rows,
            out_specs=pl.BlockSpec((2, tile, nvir), lambda m, ids: (0, m, 0)),
        ),
        compiler_params=pltpu.CompilerParams(vmem_limit_bytes=VMEM),
        cost_estimate=pl.CostEstimate(
            flops=flops, bytes_accessed=2 * naux * naux + 8 * naux * nvir, transcendentals=0
        ),
        name="transform",
    )(ids, *([metric] * count), *[array for array, _ in pieces])


def pair_kernel(ints, floats, left, before, far, row, column, amps, density, total):
    slot = pl.program_id(0)
    pair_sum = column[...] + row[...]

    @pl.when(slot == 0)
    def _():
        total[...] = jnp.zeros_like(total)

    for rnd, rights in enumerate((before, far)):
        local = ints[slot, rnd]
        right = rights[local]
        intersection = lax.dot_general(
            left[0], right, (((0,), (0,)), ((), ())), preferred_element_type=jnp.float32
        )
        gap = pair_sum - floats[0, slot] - floats[1 + rnd, local]
        kept = ints[slot, 2 + rnd].astype(jnp.float32)
        amp = (kept * intersection / gap).astype(jnp.bfloat16)
        amps[0, rnd] = amp
        total[...] += lax.dot_general(
            amp, amp, (((1,), (1,)), ((), ())), preferred_element_type=jnp.float32
        )

    @pl.when(slot == 1)
    def _():
        density[...] = total[...].astype(jnp.bfloat16)


def pairs(ints, floats, own, before, far, e_vir):
    _, naux, nvir = own.shape
    whole = pl.BlockSpec((2, naux, nvir), lambda s: (0, 0, 0))
    smem = pl.BlockSpec(memory_space=pltpu.SMEM)
    return pl.pallas_call(
        pair_kernel,
        out_shape=(
            jax.ShapeDtypeStruct((2, 2, nvir, nvir), jnp.bfloat16),
            jax.ShapeDtypeStruct((nvir, nvir), jnp.bfloat16),
        ),
        grid=(2,),
        in_specs=[
            smem,
            smem,
            pl.BlockSpec((1, naux, nvir), lambda s: (s, 0, 0)),
            whole,
            whole,
            pl.BlockSpec((1, nvir), lambda s: (0, 0)),
            pl.BlockSpec((nvir, 1), lambda s: (0, 0)),
        ],
        out_specs=(
            pl.BlockSpec((1, 2, nvir, nvir), lambda s: (s, 0, 0, 0)),
            pl.BlockSpec((nvir, nvir), lambda s: (0, 0)),
        ),
        scratch_shapes=[pltpu.VMEM((nvir, nvir), jnp.float32)],
        compiler_params=pltpu.CompilerParams(vmem_limit_bytes=VMEM),
        cost_estimate=pl.CostEstimate(
            flops=8 * naux * nvir * nvir + 8 * nvir**3,
            bytes_accessed=12 * naux * nvir,
            transcendentals=0,
        ),
        name="pairs",
    )(ints, floats, own, before, far, e_vir[None, :], e_vir[:, None])


def gradient_kernel(ints, amps, before, far, out):
    for slot in range(2):
        total = None
        for rnd, rights in enumerate((before, far)):
            term = lax.dot_general(
                rights[ints[slot, rnd]],
                amps[slot, rnd],
                (((1,), (1,)), ((), ())),
                preferred_element_type=jnp.float32,
            )
            total = term if total is None else total + term
        out[:, slot, :] = total.astype(jnp.bfloat16)


def gradient_of(ints, amps, before, far, tile=256):
    _, naux, nvir = before.shape
    rows = pl.BlockSpec((2, tile, nvir), lambda m: (0, m, 0))
    return pl.pallas_call(
        gradient_kernel,
        out_shape=jax.ShapeDtypeStruct((naux, 2, nvir), jnp.bfloat16),
        grid=(naux // tile,),
        in_specs=[
            pl.BlockSpec(memory_space=pltpu.SMEM),
            pl.BlockSpec((2, 2, nvir, nvir), lambda m: (0, 0, 0, 0)),
            rows,
            rows,
        ],
        out_specs=pl.BlockSpec((tile, 2, nvir), lambda m: (m, 0, 0)),
        compiler_params=pltpu.CompilerParams(vmem_limit_bytes=VMEM),
        cost_estimate=pl.CostEstimate(
            flops=8 * naux * nvir * nvir, bytes_accessed=12 * naux * nvir, transcendentals=0
        ),
        name="gradient",
    )(ints, amps, before, far)


def summed_at_owner(array):
    pieces = array.reshape(16, -1, array.shape[1])
    arrived = lax.all_to_all(pieces, "occ", split_axis=0, concat_axis=0, tiled=True)
    return arrived.astype(jnp.float32).sum(axis=0)


def summed_for_everyone(array):
    copies = jnp.broadcast_to(array[None], (8, *array.shape))
    arrived = lax.all_to_all(copies, "aux", 0, 0, tiled=True)
    return arrived.astype(jnp.float32).sum(axis=0)


def on_device(integrals, metric, e_occ, e_vir, partner, screen):
    nvir = integrals.shape[-1]
    device = lax.axis_index(AXES)
    aux = lax.axis_index("aux")
    y, x_hi = aux // 2, aux % 2

    by_owner = jnp.transpose(integrals, (1, 0, 2)).reshape(8, 2, ROWS, nvir)

    def block(index):
        return lax.dynamic_index_in_dim(by_owner, index, 0, True)

    def for_row(k):
        there = (y + k) % 4 * 2
        return block(there + x_hi), block(there + 1 - x_hi)

    same0, other0 = for_row(0)
    a0s = send(same0, same_hop)
    a0o = send(other0, other_hop)
    y1 = send(jnp.concatenate(for_row(1)), along_y(1))
    y3 = send(jnp.concatenate(for_row(3)), along_y(3))
    half = send(jnp.concatenate(for_row(2)), along_y(3), (y1, y3))
    same1 = jnp.concatenate([y1[:1], y3[:1]])
    other1 = jnp.concatenate([y1[1:], y3[1:]])
    a1s = send(same1, same_hop, (a0s,))
    a1o = send(other1, other_hop, (a0o,))
    even = lambda l: l & 1 == 0
    ahead = {
        k: send(block(((y + k) % 4 * 2 + 7) % 8), before_hop(k), (y1, y3), even)
        for k in (0, 1, 2, 3)
    }
    y2 = send(half, along_y(3), (a1s,))
    b1s = send(jnp.concatenate([a0o, a1o]), same_hop, (a1s,))
    b1o = send(jnp.concatenate([a0s, a1s]), onward_hop, (a1o,))
    a2s = send(y2[:1], same_hop, (b1s, b1o))
    a2o = send(y2[1:], other_hop, (b1s, b1o))
    b2s = send(a2o, same_hop)
    b2o = send(a2s, onward_hop)

    order = jnp.array([0, 1, 3, 2], jnp.int32)
    here = (y - order) % 4 * 2
    near_ids = here + x_hi
    cross_ids = here + 1 - x_hi
    late_ids = jnp.where(x_hi == 0, (here + 6) % 8 + 1, cross_ids)
    own_ids = jnp.concatenate([near_ids, cross_ids]).astype(jnp.int32)
    before_ids = jnp.concatenate([near_ids, late_ids]).astype(jnp.int32)

    far = transform(
        metric, own_ids, [(a0s, 0), (a1s, 0), (a1s, 1), (a2s, 0), (a0o, 0), (a1o, 0), (a1o, 1), (a2o, 0)]
    )
    own = transform(
        metric, own_ids, [(same0, 0), (y1, 0), (y3, 0), (y2, 0), (b1s, 0), (b1s, 1), (b1s, 2), (b2s, 0)]
    )
    near = jnp.where(
        x_hi == 0,
        jnp.concatenate([ahead[0], ahead[1], ahead[3], ahead[2]]),
        jnp.concatenate([other0, other1, y2[1:]]),
    )
    before = transform(
        metric,
        before_ids,
        [(near, 0), (near, 1), (near, 2), (near, 3), (b1o, 0), (b1o, 1), (b1o, 2), (b2o, 0)],
    )

    ints = jnp.concatenate([partner, screen], axis=1).astype(jnp.int32)
    owners = jnp.stack([device, (device - 1) % 128, (device - 64) % 128])
    floats = e_occ[owners[:, None] * 2 + jnp.arange(2)[None, :]]
    amps, density = pairs(ints, floats, own, before, far, e_vir)
    gradient = gradient_of(ints, amps, before, far)
    rows = summed_at_owner(density)
    total = summed_for_everyone(rows.astype(jnp.bfloat16))
    return gradient, total / NOCC


def solution(mesh):
    placed = (P("aux", "occ", None), P(), P(), P(), P(AXES, None), P(AXES, None))
    return jax.shard_map(
        on_device,
        mesh=mesh,
        in_specs=placed,
        out_specs=(P(None, AXES, None), P("occ", None)),
        check_vma=False,
    )
```

time: 350 us -> 252 us (0.72)
  Pallas kernels: 0 us -> 66.9 us
  waiting for transfers between devices: 139 us -> 72.1 us
  blocking collectives: 72.1 us -> 14.4 us
  starting transfers between devices: 11.5 us -> 68.7 us
  matrix products: 55.5 us -> 0 us
  local copies, waits for them, and re-layouts: 55.9 us -> 19.7 us
  loops' own time: 10.9 us -> 0 us
  other arithmetic: 3.21 us -> 8.21 us
    ppermute x2 -> x18, waiting for transfers between devices: 139 us -> 72.1 us  [send(): lax.ppermute(array, AXES, [(l, to(l)) for l in range(128) if only(l)])]
    pallas_call x0 -> x5, Pallas kernels: none -> 66.9 us  [the longest x3 43.5 us: transform(): pl.pallas_call(lambda *refs: transform_kernel(count, *refs), out_shape=ja...]
    all_to_all x2 -> x1, blocking collectives: 72.1 us -> 14.4 us  [summed_at_owner(): lax.all_to_all(pieces, 'occ', split_axis=0, concat_axis=0, tiled=True)]
    ppermute x2 -> x18, starting transfers between devices: 3.77 us -> 60.6 us  [send(): lax.ppermute(array, AXES, [(l, to(l)) for l in range(128) if only(l)])]
    dot_general x13 -> x0, matrix products: 55.5 us -> none  [the longest x4 21.4 us: one_pair(): lax.dot_general(left, right, (((0,), (0,)), ((), ())), preferred_element_...]
    while x1 -> x0, local copies, waits for them, and re-layouts: 15.2 us -> none  [on_device(): gamma, density = lax.fori_loop(0, own, visit, (gamma, density))]
    another operation x2 -> x0, loops' own time: 10.9 us -> none  [on_device(): gamma, density = lax.fori_loop(0, own, visit, (gamma, density))]
    dynamic_slice x8 -> x1, local copies, waits for them, and re-layouts: 13.1 us -> 4.44 us  [block(): return lax.dynamic_index_in_dim(by_owner, index, 0, True)]
  transfers between devices with their start and end apart: 3 -> 19, of which waited for: 2 -> 6; matrix products, arithmetic and copies ran while one was open for 14% -> 4% of each run, Pallas kernels for 0% -> 16%
where the time goes in v1:
time: 252 us; the launch traced here: 251 us
  waiting for transfers between devices  72.1 us (29%)
  starting transfers between devices  68.7 us (27%)
  Pallas kernels  66.9 us (27%)
  local copies, waits for them, and re-layouts  19.7 us (8%)
  blocking collectives  14.4 us (6%)
  other arithmetic  8.21 us (3%)
    ppermute x18, waiting for transfers between devices, send(): lax.ppermute(array, AXES, [(l, to(l)) for l in range(128) if only(l)])  72.1 us
    ppermute x18, starting transfers between devices, send(): lax.ppermute(array, AXES, [(l, to(l)) for l in range(128) if only(l)])  60.6 us
    pallas_call x3, Pallas kernels, transform(): pl.pallas_call(lambda *refs: transform_kernel(count, *refs), out_shape=ja...  43.5 us
    all_to_all x1, blocking collectives, summed_at_owner(): lax.all_to_all(pieces, 'occ', split_axis=0, concat_axis=0, tiled=True)  14.4 us
    pallas_call x1, Pallas kernels, pairs(): pl.pallas_call(pair_kernel, out_shape=(jax.ShapeDtypeStruct((2, 2, nvir,...  11.8 us
    pallas_call x1, Pallas kernels, gradient_of(): pl.pallas_call(gradient_kernel, out_shape=jax.ShapeDtypeStruct((naux, 2,...  11.5 us
    all_to_all x1, starting transfers between devices, summed_for_everyone(): arrived = lax.all_to_all(copies, 'aux', 0, 0, tiled=True)  8.15 us
    transpose x1, local copies, waits for them, and re-layouts, on_device(): by_owner = jnp.transpose(integrals, (1, 0, 2)).reshape(8, 2, ROWS, nvir)  6.54 us
  transfers between devices with their start and end apart: 19, of which 6 were waited for; matrix products, arithmetic and copies ran while one was open for 4% of the time, Pallas kernels for 16%

profile of v1, /device:TPU:4, one launch (start us, length us, event | category | flops | bytes accessed | tf_op | source)
XLA Modules:
  0.0 251.1 jit_solution(16934642575373032918)
XLA Ops:
  0.8 6.5 %copy.12 = bf16[16,256,512]{2,1,0:T(8,128)(2,1)} copy(bf16[16,256,512]{2,0,1:T(8,128)(2,1)} %bitcast.11) | data formatting | bytes 8388608 | tf_op jit(solution)/shard_map/transpose | solution.py:199
  7.4 4.4 %constant_dynamic-slice_fusion.3 = (bf16[1,2,256,512]{3,2,1,0:T(8,128)(2,1)}, bf16[1,2,256,512]{3,2,1,0:T(8,128)(2,1)}, bf16[1,2,256,512]{3,2,1,0:T(8,128)(2,1)}...) fusion(bf16[8,2,256,512]{3,2,1,0:T(8,128)(2,1)} %bitcast.10, ...), kind=kLoop, calls=%fused_computation.16 | loop fusion | bytes 12582960 | tf_op jit(solution)/shard_map/jit(dynamic_index_in_dim)/dynamic_slice | solution.py:202
  11.9 1.7 collective-permute-start
  13.7 1.7 collective-permute-start.1
  16.0 1.1 collective-permute-start.3
  17.0 21.2 %collective-permute-done.refs_10_ = bf16[2,2,256,512]{3,2,1,0:T(8,128)(2,1)S(1)} collective-permute-done((bf16[2,2,256,512]{3,2,1,0:T(8,128)(2,1)S(1)}, bf16[2,2,256,512]{3,2,1,0:T(8,128)(2,1)S(1)}, u32[]{:S(2)}, u32[]{:S(2)}) %collective-permute-start) | collective-permute-done | bytes 1048608 | tf_op jit(solution)/shard_map/ppermute | solution.py:43
  38.3 0.9 copy-done.10
  41.1 1.2 collective-permute-start.4
  42.4 2.0 collective-permute-start.2
  44.4 20.1 %collective-permute-done.7.refs_14_.refs_15_ = bf16[2,2,256,512]{3,2,1,0:T(8,128)(2,1)S(1)} collective-permute-done((bf16[2,2,256,512]{3,2,1,0:T(8,128)(2,1)S(1)}, bf16[2,2,256,512]{3,2,1,0:T(8,128)(2,1)S(1)}, u32[]{:S(2)}, u32[]{:S(2)}) %collective-permute-start.7) | collective-permute-done | bytes 1048608 | tf_op jit(solution)/shard_map/ppermute | solution.py:43
  64.5 1.4 pad_maximum_fusion
  65.9 2.5 collective-permute-start.8
  68.4 1.3 pad_maximum_fusion.1
  69.8 1.7 collective-permute-start.5
  71.6 1.5 collective-permute-start.15
  73.2 1.5 collective-permute-start.12
  74.7 19.3 %collective-permute-done.5.refs_12_ = bf16[2,2,256,512]{3,2,1,0:T(8,128)(2,1)} collective-permute-done((bf16[2,2,256,512]{3,2,1,0:T(8,128)(2,1)}, bf16[2,2,256,512]{3,2,1,0:T(8,128)(2,1)}, u32[]{:S(2)}, u32[]{:S(2)}) %collective-permute-start.5) | collective-permute-done | bytes 1048608 | tf_op jit(solution)/shard_map/ppermute | solution.py:43
  94.0 1.5 collective-permute-start.13
  95.4 5.9 %collective-permute-done.8.refs_13_.refs_14_.refs_15_ = bf16[3,2,256,512]{3,2,1,0:T(8,128)(2,1)S(1)} collective-permute-done((bf16[3,2,256,512]{3,2,1,0:T(8,128)(2,1)}, bf16[3,2,256,512]{3,2,1,0:T(8,128)(2,1)S(1)}, u32[]{:S(2)}, u32[]{:S(2)}) %collective-permute-start.8) | collective-permute-done | bytes 1572896 | tf_op jit(solution)/shard_map/ppermute | solution.py:43
  101.3 1.5 collective-permute-start.14
  105.6 1.3 fusion.5
  106.9 41.7 %collective-permute-start.10 = (bf16[1,2,256,512]{3,2,1,0:T(8,128)(2,1)S(1)}, bf16[1,2,256,512]{3,2,1,0:T(8,128)(2,1)S(1)}, u32[]{:S(2)}, u32[]{:S(2)}) collective-permute-start(bf16[1,2,256,512]{3,2,1,0:T(8,128)(2,1)S(1)} %get-tuple-element.22), channel_id=1, source_target_pairs={{0,65},{1,64},{2,67},{3,66},{4,69},{5,68},{6,71},{7,70},{8,73},{9,... | collective-permute-start | bytes 1572872 | tf_op jit(solution)/shard_map/ppermute | solution.py:43
  149.3 2.8 %maximum_select_fusion.refs_9_.refs_10_.refs_11_.refs_12_ = bf16[4,2,256,512]{3,2,1,0:T(8,128)(2,1)} fusion(bf16[1,2,256,512]{3,2,1,0:T(8,128)(2,1)} %collective-permute-done.15, bf16[1,2,256,512]{3,2,1,0:T(8,128)(2,1)} %collective-permute-done.14, bf16[1,2,256,512]{3,2,1,0:T(8,128)(2,1)} %collective-permute-done.13, ...), kind=kLoop, calls=%fused_computation.1 | loop fusion | flops 7340032 | bytes 6291457 | tf_op jit(solution)/shard_map/jit(_where)/select_n | solution.py:245
  152.1 3.6 %collective-permute-done.10.refs_16_ = bf16[1,2,256,512]{3,2,1,0:T(8,128)(2,1)S(1)} collective-permute-done((bf16[1,2,256,512]{3,2,1,0:T(8,128)(2,1)S(1)}, bf16[1,2,256,512]{3,2,1,0:T(8,128)(2,1)S(1)}, u32[]{:S(2)}, u32[]{:S(2)}) %collective-permute-start.10) | collective-permute-done | bytes 524320 | tf_op jit(solution)/shard_map/ppermute | solution.py:43
  155.7 2.0 collective-permute-done.16.refs_12_
  158.5 14.5 %transform.5.far = bf16[2,2048,512]{2,1,0:T(8,128)(2,1)} custom-call(s32[8]{0:T(128)} %get-tuple-element.51.refs_0_, bf16[2048,2048]{1,0:T(8,128)(2,1)} %refs_8_.5, bf16[2048,2048]{1,0:T(8,128)(2,1)} %refs_8_.5, bf16[2048,2048]{1,0:T(8,128)(2,1)} %refs_8_.5, bf16[2048,2048]{1,0:T(8,128)(2,1)} %refs_8_.5, bf16[2048,2048]{1,0:T(8,128)(2,1)} %refs_8_.5, ...), custom_call_target="tpu_custom_call" | custom-call | flops 8589934592 | bytes 16777216 | tf_op jit(solution)/shard_map/transform/pallas_call | solution.py:66
  173.9 14.5 %transform.3.left = bf16[2,2048,512]{2,1,0:T(8,128)(2,1)} custom-call(s32[8]{0:T(128)} %get-tuple-element.51.refs_0_, bf16[2048,2048]{1,0:T(8,128)(2,1)} %refs_8_.5, bf16[2048,2048]{1,0:T(8,128)(2,1)} %refs_8_.5, bf16[2048,2048]{1,0:T(8,128)(2,1)} %refs_8_.5, bf16[2048,2048]{1,0:T(8,128)(2,1)} %refs_8_.5, bf16[2048,2048]{1,0:T(8,128)(2,1)} %refs_8_.5, ...), custom_call_target="tpu_custom_call" | custom-call | flops 8589934592 | bytes 16777216 | tf_op jit(solution)/shard_map/transform/pallas_call | solution.py:66
  189.2 14.5 %transform.4.before = bf16[2,2048,512]{2,1,0:T(8,128)(2,1)} custom-call(s32[8]{0:T(128)} %get-tuple-element.50.refs_0_, bf16[2048,2048]{1,0:T(8,128)(2,1)} %refs_8_.5, bf16[2048,2048]{1,0:T(8,128)(2,1)} %refs_8_.5, bf16[2048,2048]{1,0:T(8,128)(2,1)} %refs_8_.5, bf16[2048,2048]{1,0:T(8,128)(2,1)} %refs_8_.5, bf16[2048,2048]{1,0:T(8,128)(2,1)} %refs_8_.5, ...), custom_call_target="tpu_custom_call" | custom-call | flops 8589934592 | bytes 16777216 | tf_op jit(solution)/shard_map/transform/pallas_call | solution.py:66
  203.7 11.8 %pairs.1 = (bf16[2,2,512,512]{3,2,1,0:T(8,128)(2,1)}, bf16[512,512]{1,0:T(8,128)(2,1)}) custom-call(s32[2,4]{1,0:T(2,128)} %pad_add_fusion.ints, f32[3,2]{1,0:T(4,128)} %reshape.79.floats, bf16[2,2048,512]{2,1,0:T(8,128)(2,1)} %transform.3.left, bf16[2,2048,512]{2,1,0:T(8,128)(2,1)} %transform.4.before, bf16[2,2048,512]{2,1,0:T(8,128)(2,1)} %transform.5.far, ...), custom_call_target="tpu_custom_call" | custom-call | flops 5368709120 | bytes 12582912 | tf_op jit(solution)/shard_map/pairs/pallas_call | solution.py:114
  215.5 14.4 %all_to_all.10 = bf16[16,32,512]{2,1,0:T(8,128)(2,1)S(1)} all-to-all(bf16[16,32,512]{2,1,0:T(8,128)(2,1)} %bitcast.12), channel_id=1, replica_groups=mesh['occ'=16,'aux'=8] {'occ'}, dimensions={0} | all-to-all | bytes 1048576 | tf_op jit(solution)/shard_map/all_to_all | solution.py:183
  230.7 8.1 %all-to-all-start.1 = ((bf16[8,32,512]{2,1,0:T(8,128)(2,1)}), bf16[8,32,512]{2,1,0:T(8,128)(2,1)S(1)}, u32[]{:S(2)}, u32[]{:S(2)}) async-start(bf16[8,32,512]{2,1,0:T(8,128)(2,1)} %broadcast_in_dim.8), calls=%async_computation.1 | async-start | bytes 524288 | tf_op jit(solution)/shard_map/all_to_all | solution.py:189
  238.9 11.5 %gradient.1 = bf16[2048,2,512]{2,1,0:T(2,128)(2,1)} custom-call(s32[2,4]{1,0:T(2,128)} %pad_add_fusion.ints, bf16[2,2,512,512]{3,2,1,0:T(8,128)(2,1)} %get-tuple-element.28.amps, bf16[2,2048,512]{2,1,0:T(8,128)(2,1)} %transform.4.before, bf16[2,2048,512]{2,1,0:T(8,128)(2,1)} %transform.5.far), custom_call_target="tpu_custom_call" | custom-call | flops 4294967296 | bytes 12582912 | tf_op jit(solution)/shard_map/gradient/pallas_call | solution.py:162
  (90 shorter events, 10.4 us)
Async XLA Ops:
  0.6 102.1 %copy-start = (f32[256]{0:T(256)S(1)}, f32[256]{0:T(256)}, u32[]{:S(2)}) copy-start(f32[256]{0:T(256)} %param.9) | copy-start | bytes 3076
  11.9 26.3 %collective-permute-start = (bf16[2,2,256,512]{3,2,1,0:T(8,128)(2,1)S(1)}, bf16[2,2,256,512]{3,2,1,0:T(8,128)(2,1)S(1)}, u32[]{:S(2)}, u32[]{:S(2)}) collective-permute-start(bf16[2,2,256,512]{3,2,1,0:T(8,128)(2,1)S(1)} %pad_maximum_fusion.2), channel_id=1, source_target_pairs={{0,2},{1,3},{2,4},{3,5},{4,6},{5,7},{6,0},{7,1},{8,10},{9,11},{10,... | collective-permute-start | bytes 3145736 | tf_op jit(solution)/shard_map/ppermute | solution.py:43
  13.7 25.5 %collective-permute-start.1 = (bf16[2,2,256,512]{3,2,1,0:T(8,128)(2,1)S(1)}, bf16[2,2,256,512]{3,2,1,0:T(8,128)(2,1)S(1)}, u32[]{:S(2)}, u32[]{:S(2)}) collective-permute-start(bf16[2,2,256,512]{3,2,1,0:T(8,128)(2,1)S(1)} %pad_maximum_fusion.3), channel_id=1, source_target_pairs={{0,6},{1,7},{2,0},{3,1},{4,2},{5,3},{6,4},{7,5},{8,14},{9,15},{10,... | collective-permute-start | bytes 3145736 | tf_op jit(solution)/shard_map/ppermute | solution.py:43
  15.4 25.0 %collective-permute-start.6 = (bf16[1,2,256,512]{3,2,1,0:T(8,128)(2,1)S(1)}, bf16[1,2,256,512]{3,2,1,0:T(8,128)(2,1)S(1)}, u32[]{:S(2)}, u32[]{:S(2)}) collective-permute-start(bf16[1,2,256,512]{3,2,1,0:T(8,128)(2,1)S(1)} %get-tuple-element.36), channel_id=1, source_target_pairs={{0,65},{1,64},{2,67},{3,66},{4,69},{5,68},{6,71},{7,70},{8,73},{9,... | collective-permute-start | bytes 1572872 | tf_op jit(solution)/shard_map/ppermute | solution.py:43
  16.0 25.1 %collective-permute-start.3 = (bf16[1,2,256,512]{3,2,1,0:T(8,128)(2,1)S(1)}, bf16[1,2,256,512]{3,2,1,0:T(8,128)(2,1)S(1)}, u32[]{:S(2)}, u32[]{:S(2)}) collective-permute-start(bf16[1,2,256,512]{3,2,1,0:T(8,128)(2,1)S(1)} %get-tuple-element.43.refs_9_), channel_id=1, source_target_pairs={{0,64},{1,65},{2,66},{3,67},{4,68},{5,69},{6,70},{7,71},{8,72},{9,... | collective-permute-start | bytes 1572872 | tf_op jit(solution)/shard_map/ppermute | solution.py:43
  40.4 24.1 %copy-start.13 = (bf16[1,2,256,512]{3,2,1,0:T(8,128)(2,1)}, bf16[1,2,256,512]{3,2,1,0:T(8,128)(2,1)S(1)}, u32[]{:S(2)}) copy-start(bf16[1,2,256,512]{3,2,1,0:T(8,128)(2,1)S(1)} %collective-permute-done.6.refs_13_) | copy-start | bytes 1572868
  40.4 24.1 %collective-permute-start.7 = (bf16[2,2,256,512]{3,2,1,0:T(8,128)(2,1)S(1)}, bf16[2,2,256,512]{3,2,1,0:T(8,128)(2,1)S(1)}, u32[]{:S(2)}, u32[]{:S(2)}) collective-permute-start(bf16[2,2,256,512]{3,2,1,0:T(8,128)(2,1)S(1)} %pad_maximum_fusion.6), channel_id=1, source_target_pairs={{0,65},{1,64},{2,67},{3,66},{4,69},{5,68},{6,71},{7,70},{8,73},{9,... | collective-permute-start | bytes 3145736 | tf_op jit(solution)/shard_map/ppermute | solution.py:43
  41.1 27.3 %copy-start.14 = (bf16[1,2,256,512]{3,2,1,0:T(8,128)(2,1)}, bf16[1,2,256,512]{3,2,1,0:T(8,128)(2,1)S(1)}, u32[]{:S(2)}) copy-start(bf16[1,2,256,512]{3,2,1,0:T(8,128)(2,1)S(1)} %collective-permute-done.3.refs_9_) | copy-start | bytes 1572868
  41.1 24.8 %collective-permute-start.4 = (bf16[2,2,256,512]{3,2,1,0:T(8,128)(2,1)S(1)}, bf16[2,2,256,512]{3,2,1,0:T(8,128)(2,1)S(1)}, u32[]{:S(2)}, u32[]{:S(2)}) collective-permute-start(bf16[2,2,256,512]{3,2,1,0:T(8,128)(2,1)S(1)} %pad_maximum_fusion.5), channel_id=1, source_target_pairs={{0,64},{1,65},{2,66},{3,67},{4,68},{5,69},{6,70},{7,71},{8,72},{9,... | collective-permute-start | bytes 3145736 | tf_op jit(solution)/shard_map/ppermute | solution.py:43
  42.4 27.4 %collective-permute-start.2 = (bf16[2,2,256,512]{3,2,1,0:T(8,128)(2,1)S(1)}, bf16[2,2,256,512]{3,2,1,0:T(8,128)(2,1)}, u32[]{:S(2)}, u32[]{:S(2)}) collective-permute-start(bf16[2,2,256,512]{3,2,1,0:T(8,128)(2,1)S(1)} %pad_maximum_fusion.4), channel_id=1, source_target_pairs={{0,6},{1,7},{2,0},{3,1},{4,2},{5,3},{6,4},{7,5},{8,14},{9,15},{10,... | collective-permute-start | bytes 3145736 | tf_op jit(solution)/shard_map/ppermute | solution.py:43
  65.9 5.7 %copy-start.24 = (s32[4]{0:T(128)S(1)}, s32[4]{0:T(128)}, u32[]{:S(2)}) copy-start(s32[4]{0:T(128)} %constant.166) | copy-start | bytes 52
  65.9 38.2 %copy-start.21 = (f32[512]{0:T(512)S(1)}, f32[512]{0:T(512)}, u32[]{:S(2)}) copy-start(f32[512]{0:T(512)} %param.10) | copy-start | bytes 6148
  65.9 39.1 %copy-start.22 = (s32[2,2]{1,0:T(2,128)S(1)}, s32[2,2]{1,0:T(2,128)}, u32[]{:S(2)}) copy-start(s32[2,2]{1,0:T(2,128)} %param.12) | copy-start | bytes 52
  65.9 39.1 %copy-start.23 = (s32[2,2]{1,0:T(2,128)S(1)}, s32[2,2]{1,0:T(2,128)}, u32[]{:S(2)}) copy-start(s32[2,2]{1,0:T(2,128)} %param.11) | copy-start | bytes 52
  65.9 35.4 %collective-permute-start.8 = (bf16[3,2,256,512]{3,2,1,0:T(8,128)(2,1)}, bf16[3,2,256,512]{3,2,1,0:T(8,128)(2,1)S(1)}, u32[]{:S(2)}, u32[]{:S(2)}) collective-permute-start(bf16[3,2,256,512]{3,2,1,0:T(8,128)(2,1)} %pad_maximum_fusion), channel_id=1, source_target_pairs={{0,64},{1,65},{2,66},{3,67},{4,68},{5,69},{6,70},{7,71},{8,72},{9,... | collective-permute-start | bytes 4718600 | tf_op jit(solution)/shard_map/ppermute | solution.py:43
  69.7 37.1 %collective-permute-start.9 = (bf16[3,2,256,512]{3,2,1,0:T(8,128)(2,1)}, bf16[3,2,256,512]{3,2,1,0:T(8,128)(2,1)S(1)}, u32[]{:S(2)}, u32[]{:S(2)}) collective-permute-start(bf16[3,2,256,512]{3,2,1,0:T(8,128)(2,1)} %pad_maximum_fusion.1), channel_id=1, source_target_pairs={{0,65},{1,66},{2,67},{3,68},{4,69},{5,70},{6,71},{7,72},{8,73},{9,... | collective-permute-start | bytes 4718600 | tf_op jit(solution)/shard_map/ppermute | solution.py:43
  69.8 24.2 %collective-permute-start.5 = (bf16[2,2,256,512]{3,2,1,0:T(8,128)(2,1)}, bf16[2,2,256,512]{3,2,1,0:T(8,128)(2,1)}, u32[]{:S(2)}, u32[]{:S(2)}) collective-permute-start(bf16[2,2,256,512]{3,2,1,0:T(8,128)(2,1)} %collective-permute-done.2), channel_id=1, source_target_pairs={{0,6},{1,7},{2,0},{3,1},{4,2},{5,3},{6,4},{7,5},{8,14},{9,15},{10,... | collective-permute-start | bytes 3145736 | tf_op jit(solution)/shard_map/ppermute | solution.py:43
  71.6 76.9 %collective-permute-start.15 = (bf16[1,2,256,512]{3,2,1,0:T(8,128)(2,1)}, bf16[1,2,256,512]{3,2,1,0:T(8,128)(2,1)}, u32[]{:S(2)}, u32[]{:S(2)}) collective-permute-start(bf16[1,2,256,512]{3,2,1,0:T(8,128)(2,1)} %get-tuple-element.26), channel_id=1, source_target_pairs={{0,4},{2,6},{4,8},{6,2},{8,12},{10,14},{12,16},{14,10},{16,20},{18... | collective-permute-start | bytes 1572872 | tf_op jit(solution)/shard_map/ppermute | solution.py:43
  73.2 76.0 %collective-permute-start.12 = (bf16[1,2,256,512]{3,2,1,0:T(8,128)(2,1)}, bf16[1,2,256,512]{3,2,1,0:T(8,128)(2,1)}, u32[]{:S(2)}, u32[]{:S(2)}) collective-permute-start(bf16[1,2,256,512]{3,2,1,0:T(8,128)(2,1)} %get-tuple-element.23), channel_id=1, source_target_pairs={{0,8},{2,2},{4,4},{6,6},{8,16},{10,10},{12,12},{14,14},{16,24},{18... | collective-permute-start | bytes 1572872 | tf_op jit(solution)/shard_map/ppermute | solution.py:43
  94.0 55.3 %collective-permute-start.13 = (bf16[1,2,256,512]{3,2,1,0:T(8,128)(2,1)}, bf16[1,2,256,512]{3,2,1,0:T(8,128)(2,1)}, u32[]{:S(2)}, u32[]{:S(2)}) collective-permute-start(bf16[1,2,256,512]{3,2,1,0:T(8,128)(2,1)} %get-tuple-element.24), channel_id=1, source_target_pairs={{0,2},{2,4},{4,6},{6,8},{8,10},{10,12},{12,14},{14,16},{16,18},{18... | collective-permute-start | bytes 1572872 | tf_op jit(solution)/shard_map/ppermute | solution.py:43
  101.3 5.5 %copy-start.3 = (bf16[3,2,256,512]{3,2,1,0:T(8,128)(2,1)}, bf16[3,2,256,512]{3,2,1,0:T(8,128)(2,1)S(1)}, u32[]{:S(2)}) copy-start(bf16[3,2,256,512]{3,2,1,0:T(8,128)(2,1)S(1)} %collective-permute-done.8.refs_13_.refs_14_.refs_15_) | copy-start | bytes 4718596
  101.3 47.9 %collective-permute-start.14 = (bf16[1,2,256,512]{3,2,1,0:T(8,128)(2,1)}, bf16[1,2,256,512]{3,2,1,0:T(8,128)(2,1)}, u32[]{:S(2)}, u32[]{:S(2)}) collective-permute-start(bf16[1,2,256,512]{3,2,1,0:T(8,128)(2,1)} %get-tuple-element.25), channel_id=1, source_target_pairs={{0,6},{2,8},{4,2},{6,4},{8,14},{10,16},{12,10},{14,12},{16,22},{18... | collective-permute-start | bytes 1572872 | tf_op jit(solution)/shard_map/ppermute | solution.py:43
  105.0 44.3 %copy-start.7 = (bf16[1,2,256,512]{3,2,1,0:T(8,128)(2,1)S(1)}, bf16[1,2,256,512]{3,2,1,0:T(8,128)(2,1)}, u32[]{:S(2)}) copy-start(bf16[1,2,256,512]{3,2,1,0:T(8,128)(2,1)} %copy-done.6) | copy-start | bytes 1572868
  105.0 44.3 %copy-start.9 = (bf16[1,2,256,512]{3,2,1,0:T(8,128)(2,1)S(1)}, bf16[1,2,256,512]{3,2,1,0:T(8,128)(2,1)}, u32[]{:S(2)}) copy-start(bf16[1,2,256,512]{3,2,1,0:T(8,128)(2,1)} %copy-done.8) | copy-start | bytes 1572868
  105.0 44.3 %copy-start.16 = (bf16[1,2,256,512]{3,2,1,0:T(8,128)(2,1)S(1)}, bf16[1,2,256,512]{3,2,1,0:T(8,128)(2,1)}, u32[]{:S(2)}) copy-start(bf16[1,2,256,512]{3,2,1,0:T(8,128)(2,1)} %copy-done.15) | copy-start | bytes 1572868
  106.9 45.2 %copy-start.2 = (bf16[3,2,256,512]{3,2,1,0:T(8,128)(2,1)}, bf16[3,2,256,512]{3,2,1,0:T(8,128)(2,1)S(1)}, u32[]{:S(2)}) copy-start(bf16[3,2,256,512]{3,2,1,0:T(8,128)(2,1)S(1)} %collective-permute-done.9.refs_13_.refs_14_.refs_15_) | copy-start | bytes 4718596
  106.9 48.9 %collective-permute-start.10 = (bf16[1,2,256,512]{3,2,1,0:T(8,128)(2,1)S(1)}, bf16[1,2,256,512]{3,2,1,0:T(8,128)(2,1)S(1)}, u32[]{:S(2)}, u32[]{:S(2)}) collective-permute-start(bf16[1,2,256,512]{3,2,1,0:T(8,128)(2,1)S(1)} %get-tuple-element.22), channel_id=1, source_target_pairs={{0,65},{1,64},{2,67},{3,66},{4,69},{5,68},{6,71},{7,70},{8,73},{9,... | collective-permute-start | bytes 1572872 | tf_op jit(solution)/shard_map/ppermute | solution.py:43
  148.6 9.2 %collective-permute-start.16 = (bf16[1,2,256,512]{3,2,1,0:T(8,128)(2,1)S(1)}, bf16[1,2,256,512]{3,2,1,0:T(8,128)(2,1)S(1)}, u32[]{:S(2)}, u32[]{:S(2)}) collective-permute-start(bf16[1,2,256,512]{3,2,1,0:T(8,128)(2,1)S(1)} %get-tuple-element.27), channel_id=1, source_target_pairs={{0,64},{1,65},{2,66},{3,67},{4,68},{5,69},{6,70},{7,71},{8,72},{9,... | collective-permute-start | bytes 1572872 | tf_op jit(solution)/shard_map/ppermute | solution.py:43
  155.7 17.3 %collective-permute-start.11 = (bf16[1,2,256,512]{3,2,1,0:T(8,128)(2,1)S(1)}, bf16[1,2,256,512]{3,2,1,0:T(8,128)(2,1)S(1)}, u32[]{:S(2)}, u32[]{:S(2)}) collective-permute-start(bf16[1,2,256,512]{3,2,1,0:T(8,128)(2,1)S(1)} %collective-permute-done.10.refs_16_), channel_id=1, source_target_pairs={{0,64},{1,65},{2,66},{3,67},{4,68},{5,69},{6,70},{7,71},{8,72},{9,... | collective-permute-start | bytes 1572872 | tf_op jit(solution)/shard_map/ppermute | solution.py:43
  157.7 30.6 %collective-permute-start.17 = (bf16[1,2,256,512]{3,2,1,0:T(8,128)(2,1)S(1)}, bf16[1,2,256,512]{3,2,1,0:T(8,128)(2,1)S(1)}, u32[]{:S(2)}, u32[]{:S(2)}) collective-permute-start(bf16[1,2,256,512]{3,2,1,0:T(8,128)(2,1)S(1)} %collective-permute-done.16.refs_12_), channel_id=1, source_target_pairs={{0,65},{1,66},{2,67},{3,68},{4,69},{5,70},{6,71},{7,72},{8,73},{9,... | collective-permute-start | bytes 1572872 | tf_op jit(solution)/shard_map/ppermute | solution.py:43
  230.7 19.7 %all-to-all-start.1 = ((bf16[8,32,512]{2,1,0:T(8,128)(2,1)}), bf16[8,32,512]{2,1,0:T(8,128)(2,1)S(1)}, u32[]{:S(2)}, u32[]{:S(2)}) async-start(bf16[8,32,512]{2,1,0:T(8,128)(2,1)} %broadcast_in_dim.8), calls=%async_computation.1 | async-start | bytes 524288 | tf_op jit(solution)/shard_map/all_to_all | solution.py:189
  238.9 12.2 %copy-start.1 = (f32[256]{0:T(256)S(1)}, f32[256]{0:T(256)}, u32[]{:S(2)}) copy-start(f32[256]{0:T(256)} %param.9) | copy-start | bytes 3076
  (12 other events, 25.9 us)

commit v2 on v1

--- a/solution.py
+++ b/solution.py
@@ -49,35 +49,44 @@
     for slot in range(2):
         right = jnp.concatenate([ref[slot] for ref in refs[count : 2 * count]], axis=0)
         mixed = jnp.dot(metric, right, preferred_element_type=jnp.float32)
+        if len(refs) == 2 * count + 2:
+            mixed = mixed + refs[2 * count][slot]
         out[slot] = mixed.astype(out.dtype)
 
 
-def transform(metric, ids, pieces, tile=512):
+def transform(metric, ids, pieces, sofar=None, dtype=jnp.bfloat16, tile=512):
     count = len(pieces)
     naux = metric.shape[0]
     nvir = pieces[0][0].shape[-1]
     columns = [
-        pl.BlockSpec((tile, ROWS), lambda m, ids, k=k: (m, ids[k])) for k in range(count)
+        pl.BlockSpec((tile, ROWS), lambda m, ids, k=k: (m, ids[k])) for _, _, k in pieces
     ]
     rows = [
-        pl.BlockSpec((None, 2, ROWS, nvir), lambda m, ids, n=n: (n, 0, 0, 0)) for _, n in pieces
+        pl.BlockSpec((None, 2, ROWS, nvir), lambda m, ids, n=n: (n, 0, 0, 0))
+        for _, n, _ in pieces
     ]
-    flops = 2 * naux * count * ROWS * 2 * nvir
+    sums = pl.BlockSpec((2, tile, nvir), lambda m, ids: (0, m, 0))
+    flops = 4 * naux * count * ROWS * nvir
+    moved = 2 * naux * count * ROWS + 4 * count * ROWS * nvir
+    moved += 2 * naux * nvir * ((4 if sofar is not None else 0) + jnp.dtype(dtype).itemsize)
     return pl.pallas_call(
         lambda *refs: transform_kernel(count, *refs),
-        out_shape=jax.ShapeDtypeStruct((2, naux, nvir), jnp.bfloat16),
+        out_shape=jax.ShapeDtypeStruct((2, naux, nvir), dtype),
         grid_spec=pltpu.PrefetchScalarGridSpec(
             num_scalar_prefetch=1,
             grid=(naux // tile,),
-            in_specs=columns + rows,
-            out_specs=pl.BlockSpec((2, tile, nvir), lambda m, ids: (0, m, 0)),
+            in_specs=columns + rows + ([] if sofar is None else [sums]),
+            out_specs=sums,
         ),
         compiler_params=pltpu.CompilerParams(vmem_limit_bytes=VMEM),
-        cost_estimate=pl.CostEstimate(
-            flops=flops, bytes_accessed=2 * naux * naux + 8 * naux * nvir, transcendentals=0
-        ),
+        cost_estimate=pl.CostEstimate(flops=flops, bytes_accessed=moved, transcendentals=0),
         name="transform",
-    )(ids, *([metric] * count), *[array for array, _ in pieces])
+    )(
+        ids,
+        *([metric] * count),
+        *[array for array, _, _ in pieces],
+        *([] if sofar is None else [sofar]),
+    )
 
 
 def pair_kernel(ints, floats, left, before, far, row, column, amps, density, total):
@@ -210,19 +219,21 @@
     a0o = send(other0, other_hop)
     y1 = send(jnp.concatenate(for_row(1)), along_y(1))
     y3 = send(jnp.concatenate(for_row(3)), along_y(3))
-    half = send(jnp.concatenate(for_row(2)), along_y(3), (y1, y3))
+    third = jnp.concatenate(for_row(2))
+    even = lambda l: l & 1 == 0
+    block_ahead = {k: block(((y + k) % 4 * 2 + 7) % 8) for k in range(4)}
+    y1, y3, a0s, a0o, third, block_ahead = lax.optimization_barrier(
+        (y1, y3, a0s, a0o, third, block_ahead)
+    )
+    half = send(third, along_y(3))
     same1 = jnp.concatenate([y1[:1], y3[:1]])
     other1 = jnp.concatenate([y1[1:], y3[1:]])
-    a1s = send(same1, same_hop, (a0s,))
-    a1o = send(other1, other_hop, (a0o,))
-    even = lambda l: l & 1 == 0
-    ahead = {
-        k: send(block(((y + k) % 4 * 2 + 7) % 8), before_hop(k), (y1, y3), even)
-        for k in (0, 1, 2, 3)
-    }
+    a1s = send(same1, same_hop)
+    a1o = send(other1, other_hop)
+    ahead = {k: send(block_ahead[k], before_hop(k), (), even) for k in range(4)}
     y2 = send(half, along_y(3), (a1s,))
-    b1s = send(jnp.concatenate([a0o, a1o]), same_hop, (a1s,))
-    b1o = send(jnp.concatenate([a0s, a1s]), onward_hop, (a1o,))
+    b1s = send(jnp.concatenate([a0o, a1o]), same_hop, (a1s, *ahead.values()))
+    b1o = send(jnp.concatenate([a0s, a1s]), onward_hop, (a1o, *ahead.values()))
     a2s = send(y2[:1], same_hop, (b1s, b1o))
     a2o = send(y2[1:], other_hop, (b1s, b1o))
     b2s = send(a2o, same_hop)
@@ -236,11 +247,18 @@
     own_ids = jnp.concatenate([near_ids, cross_ids]).astype(jnp.int32)
     before_ids = jnp.concatenate([near_ids, late_ids]).astype(jnp.int32)
 
+    wide = jnp.float32
     far = transform(
-        metric, own_ids, [(a0s, 0), (a1s, 0), (a1s, 1), (a2s, 0), (a0o, 0), (a1o, 0), (a1o, 1), (a2o, 0)]
+        metric,
+        own_ids,
+        [(a0s, 0, 0), (a1s, 0, 1), (a1s, 1, 2), (a0o, 0, 4), (a1o, 0, 5), (a1o, 1, 6)],
+        dtype=wide,
     )
     own = transform(
-        metric, own_ids, [(same0, 0), (y1, 0), (y3, 0), (y2, 0), (b1s, 0), (b1s, 1), (b1s, 2), (b2s, 0)]
+        metric,
+        own_ids,
+        [(same0, 0, 0), (y1, 0, 1), (y3, 0, 2), (y2, 0, 3), (b1s, 0, 4), (b1s, 1, 5), (b1s, 2, 6)],
+        dtype=wide,
     )
     near = jnp.where(
         x_hi == 0,
@@ -250,8 +268,12 @@
     before = transform(
         metric,
         before_ids,
-        [(near, 0), (near, 1), (near, 2), (near, 3), (b1o, 0), (b1o, 1), (b1o, 2), (b2o, 0)],
-    )
+        [(near, k, k) for k in range(4)] + [(b1o, k, 4 + k) for k in range(3)],
+        dtype=wide,
+    )
+    far = transform(metric, own_ids, [(a2s, 0, 3), (a2o, 0, 7)], far)
+    own = transform(metric, own_ids, [(b2s, 0, 7)], own)
+    before = transform(metric, before_ids, [(b2o, 0, 7)], before)
 
     ints = jnp.concatenate([partner, screen], axis=1).astype(jnp.int32)
     owners = jnp.stack([device, (device - 1) % 128, (device - 64) % 128])

time: 252 us -> 254 us (level)
  waiting for transfers between devices: 72.1 us -> 50.4 us
  Pallas kernels: 66.9 us -> 86.5 us
  starting transfers between devices: 68.7 us -> 50.6 us
  blocking collectives: 14.4 us -> 31.7 us
  other arithmetic: 8.21 us -> 13.3 us
    ppermute x18, waiting for transfers between devices: 72.1 us -> 50.4 us  [send(): lax.ppermute(array, AXES, [(l, to(l)) for l in range(128) if only(l)])]
    pallas_call x3 -> x6, Pallas kernels: 43.5 us -> 63.1 us  [transform(): pl.pallas_call(lambda *refs: transform_kernel(count, *refs), out_shape=ja...]
    all_to_all x1, blocking collectives: 14.4 us -> 31.7 us  [summed_at_owner(): lax.all_to_all(pieces, 'occ', split_axis=0, concat_axis=0, tiled=True)]
    ppermute x18, starting transfers between devices: 60.6 us -> 43.5 us  [send(): lax.ppermute(array, AXES, [(l, to(l)) for l in range(128) if only(l)])]
    concatenate x3, other arithmetic: 2.81 us -> 5.73 us  [the longest x1 2.33 us: on_device(): b1o = send(jnp.concatenate([a0s, a1s]), onward_hop, (a1o, *ahead.values()))]
  transfers between devices with their start and end apart: 19 -> 19, of which waited for: 6 -> 7; matrix products, arithmetic and copies ran while one was open for 4% -> 7% of each run, Pallas kernels for 16% -> 27%
where the time goes in v2:
time: 254 us; the launch traced here: 253 us
  Pallas kernels  86.5 us (34%)
  starting transfers between devices  50.6 us (20%)
  waiting for transfers between devices  50.4 us (20%)
  blocking collectives  31.7 us (12%)
  local copies, waits for them, and re-layouts  19.1 us (8%)
  other arithmetic  13.3 us (5%)
    pallas_call x6, Pallas kernels, transform(): pl.pallas_call(lambda *refs: transform_kernel(count, *refs), out_shape=ja...  63.1 us
    ppermute x18, waiting for transfers between devices, send(): lax.ppermute(array, AXES, [(l, to(l)) for l in range(128) if only(l)])  50.4 us
    ppermute x18, starting transfers between devices, send(): lax.ppermute(array, AXES, [(l, to(l)) for l in range(128) if only(l)])  43.5 us
    all_to_all x1, blocking collectives, summed_at_owner(): lax.all_to_all(pieces, 'occ', split_axis=0, concat_axis=0, tiled=True)  31.7 us
    pallas_call x1, Pallas kernels, pairs(): pl.pallas_call(pair_kernel, out_shape=(jax.ShapeDtypeStruct((2, 2, nvir,...  11.9 us
    pallas_call x1, Pallas kernels, gradient_of(): pl.pallas_call(gradient_kernel, out_shape=jax.ShapeDtypeStruct((naux, 2,...  11.5 us
    all_to_all x1, starting transfers between devices, summed_for_everyone(): arrived = lax.all_to_all(copies, 'aux', 0, 0, tiled=True)  7.18 us
    transpose x1, local copies, waits for them, and re-layouts, on_device(): by_owner = jnp.transpose(integrals, (1, 0, 2)).reshape(8, 2, ROWS, nvir)  6.54 us
  transfers between devices with their start and end apart: 19, of which 7 were waited for; matrix products, arithmetic and copies ran while one was open for 7% of the time, Pallas kernels for 27%

profile of v2, /device:TPU:4, one launch (start us, length us, event | category | flops | bytes accessed | tf_op | source)
XLA Modules:
  0.0 252.6 jit_solution(1955979731787631455)
XLA Ops:
  0.8 6.5 %copy.12 = bf16[16,256,512]{2,1,0:T(8,128)(2,1)} copy(bf16[16,256,512]{2,0,1:T(8,128)(2,1)} %bitcast.11) | data formatting | bytes 8388608 | tf_op jit(solution)/shard_map/transpose | solution.py:208
  7.4 4.5 %constant_dynamic-slice_fusion = (bf16[1,2,256,512]{3,2,1,0:T(8,128)(2,1)}, bf16[1,2,256,512]{3,2,1,0:T(8,128)(2,1)}, bf16[1,2,256,512]{3,2,1,0:T(8,128)(2,1)}, ...) fusion(bf16[8,2,256,512]{3,2,1,0:T(8,128)(2,1)} %bitcast.10, ...), kind=kLoop, calls=%fused_computation.13 | loop fusion | bytes 12582960 | tf_op jit(solution)/shard_map/jit(dynamic_index_in_dim)/dynamic_slice | solution.py:211
  12.0 1.6 collective-permute-start
  13.7 1.7 collective-permute-start.1
  18.0 10.7 %collective-permute-done.3.refs_10_ = bf16[1,2,256,512]{3,2,1,0:T(8,128)(2,1)} collective-permute-done((bf16[1,2,256,512]{3,2,1,0:T(8,128)(2,1)S(1)}, bf16[1,2,256,512]{3,2,1,0:T(8,128)(2,1)}, u32[]{:S(2)}, u32[]{:S(2)}) %collective-permute-start.3) | collective-permute-done | bytes 524320 | tf_op jit(solution)/shard_map/ppermute | solution.py:43
  29.0 9.2 %collective-permute-done.refs_9_ = bf16[2,2,256,512]{3,2,1,0:T(8,128)(2,1)S(1)} collective-permute-done((bf16[2,2,256,512]{3,2,1,0:T(8,128)(2,1)S(1)}, bf16[2,2,256,512]{3,2,1,0:T(8,128)(2,1)S(1)}, u32[]{:S(2)}, u32[]{:S(2)}) %collective-permute-start) | collective-permute-done | bytes 1048608 | tf_op jit(solution)/shard_map/ppermute | solution.py:43
  38.4 2.9 %collective-permute-start.4 = (bf16[2,2,256,512]{3,2,1,0:T(8,128)(2,1)}, bf16[2,2,256,512]{3,2,1,0:T(8,128)(2,1)}, u32[]{:S(2)}, u32[]{:S(2)}) collective-permute-start(bf16[2,2,256,512]{3,2,1,0:T(8,128)(2,1)} %pad_maximum_fusion.4), channel_id=1, source_target_pairs={{0,6},{1,7},{2,0},{3,1},{4,2},{5,3},{6,4},{7,5},{8,14},{9,15},{10,... | collective-permute-start | bytes 3145736 | tf_op jit(solution)/shard_map/ppermute | solution.py:43
  45.2 1.4 collective-permute-start.8
  46.6 1.5 collective-permute-start.9
  48.1 14.8 %collective-permute-done.4 = bf16[2,2,256,512]{3,2,1,0:T(8,128)(2,1)} collective-permute-done((bf16[2,2,256,512]{3,2,1,0:T(8,128)(2,1)}, bf16[2,2,256,512]{3,2,1,0:T(8,128)(2,1)}, u32[]{:S(2)}, u32[]{:S(2)}) %collective-permute-start.4) | collective-permute-done | bytes 1048608 | tf_op jit(solution)/shard_map/ppermute | solution.py:43
  62.9 1.4 collective-permute-start.10
  64.4 2.0 collective-permute-done.5.refs_8_.refs_9_
  66.3 1.4 collective-permute-start.11
  70.6 2.3 pad_maximum_fusion.1
  73.0 1.7 collective-permute-start.6
  75.7 2.3 pad_maximum_fusion
  79.2 18.1 %collective-permute-start.13 = (bf16[3,2,256,512]{3,2,1,0:T(8,128)(2,1)}, bf16[3,2,256,512]{3,2,1,0:T(8,128)(2,1)S(1)}, u32[]{:S(2)}, u32[]{:S(2)}) collective-permute-start(bf16[3,2,256,512]{3,2,1,0:T(8,128)(2,1)} %pad_maximum_fusion.1), channel_id=1, source_target_pairs={{0,65},{1,66},{2,67},{3,68},{4,69},{5,70},{6,71},{7,72},{8,73},{9,... | collective-permute-start | bytes 4718600 | tf_op jit(solution)/shard_map/ppermute | solution.py:43
  98.0 12.4 %transform.10.refs_5_ = f32[2,2048,512]{2,1,0:T(8,128)} custom-call(s32[8]{0:T(128)} %get-tuple-element.55.refs_0_, bf16[2048,2048]{1,0:T(8,128)(2,1)} %refs_2_.7, bf16[2048,2048]{1,0:T(8,128)(2,1)} %refs_2_.7, bf16[2048,2048]{1,0:T(8,128)(2,1)} %refs_2_.7, bf16[2048,2048]{1,0:T(8,128)(2,1)} %refs_2_.7, bf16[2048,2048]{1,0:T(8,128)(2,1)} %refs_2_.7, ...), custom_call_target="tpu_custom_call" | custom-call | flops 6442450944 | bytes 17825792 | tf_op jit(solution)/shard_map/transform/pallas_call | solution.py:72
  110.4 2.3 fusion.5
  112.8 2.9 %maximum_select_fusion.refs_8_.refs_9_.refs_10_.refs_11_ = bf16[4,2,256,512]{3,2,1,0:T(8,128)(2,1)} fusion(bf16[1,2,256,512]{3,2,1,0:T(8,128)(2,1)} %collective-permute-done.10, bf16[1,2,256,512]{3,2,1,0:T(8,128)(2,1)} %collective-permute-done.11, bf16[1,2,256,512]{3,2,1,0:T(8,128)(2,1)} %collective-permute-done.9, ...), kind=kLoop, calls=%fused_computation.1 | loop fusion | flops 7340032 | bytes 6291457 | tf_op jit(solution)/shard_map/jit(_where)/select_n | solution.py:263
  115.7 13.2 %collective-permute-done.13.refs_12_.refs_13_.refs_14_ = bf16[3,2,256,512]{3,2,1,0:T(8,128)(2,1)S(1)} collective-permute-done((bf16[3,2,256,512]{3,2,1,0:T(8,128)(2,1)}, bf16[3,2,256,512]{3,2,1,0:T(8,128)(2,1)S(1)}, u32[]{:S(2)}, u32[]{:S(2)}) %collective-permute-start.13) | collective-permute-done | bytes 1572896 | tf_op jit(solution)/shard_map/ppermute | solution.py:43
  128.9 4.8 %collective-permute-start.14 = (bf16[1,2,256,512]{3,2,1,0:T(8,128)(2,1)}, bf16[1,2,256,512]{3,2,1,0:T(8,128)(2,1)}, u32[]{:S(2)}, u32[]{:S(2)}) collective-permute-start(bf16[1,2,256,512]{3,2,1,0:T(8,128)(2,1)} %get-tuple-element.30), channel_id=1, source_target_pairs={{0,65},{1,64},{2,67},{3,66},{4,69},{5,68},{6,71},{7,70},{8,73},{9,... | collective-permute-start | bytes 1572872 | tf_op jit(solution)/shard_map/ppermute | solution.py:43
  133.7 2.4 collective-permute-start.16
  136.1 13.6 %transform.6.refs_3_ = f32[2,2048,512]{2,1,0:T(8,128)} custom-call(s32[8]{0:T(128)} %get-tuple-element.55.refs_0_, bf16[2048,2048]{1,0:T(8,128)(2,1)} %refs_2_.7, bf16[2048,2048]{1,0:T(8,128)(2,1)} %refs_2_.7, bf16[2048,2048]{1,0:T(8,128)(2,1)} %refs_2_.7, bf16[2048,2048]{1,0:T(8,128)(2,1)} %refs_2_.7, bf16[2048,2048]{1,0:T(8,128)(2,1)} %refs_2_.7, ...), custom_call_target="tpu_custom_call" | custom-call | flops 7516192768 | bytes 19398656 | tf_op jit(solution)/shard_map/transform/pallas_call | solution.py:72
  150.0 13.7 %transform.8.refs_3_ = f32[2,2048,512]{2,1,0:T(8,128)} custom-call(s32[8]{0:T(128)} %get-tuple-element.54.refs_0_, bf16[2048,2048]{1,0:T(8,128)(2,1)} %refs_2_.7, bf16[2048,2048]{1,0:T(8,128)(2,1)} %refs_2_.7, bf16[2048,2048]{1,0:T(8,128)(2,1)} %refs_2_.7, bf16[2048,2048]{1,0:T(8,128)(2,1)} %refs_2_.7, bf16[2048,2048]{1,0:T(8,128)(2,1)} %refs_2_.7, ...), custom_call_target="tpu_custom_call" | custom-call | flops 7516192768 | bytes 19398656 | tf_op jit(solution)/shard_map/transform/pallas_call | solution.py:72
  163.7 8.5 %transform.11.far = bf16[2,2048,512]{2,1,0:T(8,128)(2,1)} custom-call(s32[8]{0:T(128)} %get-tuple-element.55.refs_0_, bf16[2048,2048]{1,0:T(8,128)(2,1)} %refs_2_.7, bf16[2048,2048]{1,0:T(8,128)(2,1)} %refs_2_.7, bf16[1,2,256,512]{3,2,1,0:T(8,128)(2,1)} %copy-done.13, bf16[1,2,256,512]{3,2,1,0:T(8,128)(2,1)} %collective-permute-done.14.refs_4_, ...), custom_call_target="tpu_custom_call" | custom-call | flops 2147483648 | bytes 15728640 | tf_op jit(solution)/shard_map/transform/pallas_call | solution.py:72
  173.0 7.5 %transform.7.left = bf16[2,2048,512]{2,1,0:T(8,128)(2,1)} custom-call(s32[8]{0:T(128)} %get-tuple-element.55.refs_0_, bf16[2048,2048]{1,0:T(8,128)(2,1)} %refs_2_.7, bf16[1,2,256,512]{3,2,1,0:T(8,128)(2,1)} %copy-done.14, f32[2,2048,512]{2,1,0:T(8,128)} %transform.6.refs_3_), custom_call_target="tpu_custom_call" | custom-call | flops 1073741824 | bytes 14155776 | tf_op jit(solution)/shard_map/transform/pallas_call | solution.py:72
  181.3 7.5 %transform.9.before = bf16[2,2048,512]{2,1,0:T(8,128)(2,1)} custom-call(s32[8]{0:T(128)} %get-tuple-element.54.refs_0_, bf16[2048,2048]{1,0:T(8,128)(2,1)} %refs_2_.7, bf16[1,2,256,512]{3,2,1,0:T(8,128)(2,1)} %copy-done.15, f32[2,2048,512]{2,1,0:T(8,128)} %transform.8.refs_3_), custom_call_target="tpu_custom_call" | custom-call | flops 1073741824 | bytes 14155776 | tf_op jit(solution)/shard_map/transform/pallas_call | solution.py:72
  188.8 11.9 %pairs.1 = (bf16[2,2,512,512]{3,2,1,0:T(8,128)(2,1)}, bf16[512,512]{1,0:T(8,128)(2,1)}) custom-call(s32[2,4]{1,0:T(2,128)} %pad_add_fusion.ints, f32[3,2]{1,0:T(4,128)} %reshape.79.floats, bf16[2,2048,512]{2,1,0:T(8,128)(2,1)} %transform.7.left, bf16[2,2048,512]{2,1,0:T(8,128)(2,1)} %transform.9.before, bf16[2,2048,512]{2,1,0:T(8,128)(2,1)} %transform.11.far, ...), custom_call_target="tpu_custom_call" | custom-call | flops 5368709120 | bytes 12582912 | tf_op jit(solution)/shard_map/pairs/pallas_call | solution.py:123
  200.7 31.7 %all_to_all.10 = bf16[16,32,512]{2,1,0:T(8,128)(2,1)S(1)} all-to-all(bf16[16,32,512]{2,1,0:T(8,128)(2,1)} %bitcast.12), channel_id=1, replica_groups=mesh['occ'=16,'aux'=8] {'occ'}, dimensions={0} | all-to-all | bytes 1048576 | tf_op jit(solution)/shard_map/all_to_all | solution.py:192
  233.2 7.2 %all-to-all-start.1 = ((bf16[8,32,512]{2,1,0:T(8,128)(2,1)}), bf16[8,32,512]{2,1,0:T(8,128)(2,1)S(1)}, u32[]{:S(2)}, u32[]{:S(2)}) async-start(bf16[8,32,512]{2,1,0:T(8,128)(2,1)} %broadcast_in_dim.8), calls=%async_computation.1 | async-start | bytes 524288 | tf_op jit(solution)/shard_map/all_to_all | solution.py:198
  240.4 11.5 %gradient.1 = bf16[2048,2,512]{2,1,0:T(2,128)(2,1)} custom-call(s32[2,4]{1,0:T(2,128)} %pad_add_fusion.ints, bf16[2,2,512,512]{3,2,1,0:T(8,128)(2,1)} %get-tuple-element.32.amps, bf16[2,2048,512]{2,1,0:T(8,128)(2,1)} %transform.9.before, bf16[2,2048,512]{2,1,0:T(8,128)(2,1)} %transform.11.far), custom_call_target="tpu_custom_call" | custom-call | flops 4294967296 | bytes 12582912 | tf_op jit(solution)/shard_map/gradient/pallas_call | solution.py:171
  (82 shorter events, 16.2 us)
Async XLA Ops:
  0.6 67.1 %copy-start = (f32[256]{0:T(256)S(1)}, f32[256]{0:T(256)}, u32[]{:S(2)}) copy-start(f32[256]{0:T(256)} %param.9) | copy-start | bytes 3076
  11.9 3.6 %copy-start.11 = (bf16[1,2,256,512]{3,2,1,0:T(8,128)(2,1)}, bf16[1,2,256,512]{3,2,1,0:T(8,128)(2,1)S(1)}, u32[]{:S(2)}) copy-start(bf16[1,2,256,512]{3,2,1,0:T(8,128)(2,1)S(1)} %get-tuple-element.42) | copy-start | bytes 1572868
  11.9 4.1 %copy-start.10 = (bf16[1,2,256,512]{3,2,1,0:T(8,128)(2,1)}, bf16[1,2,256,512]{3,2,1,0:T(8,128)(2,1)S(1)}, u32[]{:S(2)}) copy-start(bf16[1,2,256,512]{3,2,1,0:T(8,128)(2,1)S(1)} %get-tuple-element.43.refs_8_) | copy-start | bytes 1572868
  12.0 26.2 %collective-permute-start = (bf16[2,2,256,512]{3,2,1,0:T(8,128)(2,1)S(1)}, bf16[2,2,256,512]{3,2,1,0:T(8,128)(2,1)S(1)}, u32[]{:S(2)}, u32[]{:S(2)}) collective-permute-start(bf16[2,2,256,512]{3,2,1,0:T(8,128)(2,1)S(1)} %pad_maximum_fusion.2), channel_id=1, source_target_pairs={{0,2},{1,3},{2,4},{3,5},{4,6},{5,7},{6,0},{7,1},{8,10},{9,11},{10,... | collective-permute-start | bytes 3145736 | tf_op jit(solution)/shard_map/ppermute | solution.py:43
  13.7 24.7 %collective-permute-start.1 = (bf16[2,2,256,512]{3,2,1,0:T(8,128)(2,1)S(1)}, bf16[2,2,256,512]{3,2,1,0:T(8,128)(2,1)S(1)}, u32[]{:S(2)}, u32[]{:S(2)}) collective-permute-start(bf16[2,2,256,512]{3,2,1,0:T(8,128)(2,1)S(1)} %pad_maximum_fusion.3), channel_id=1, source_target_pairs={{0,6},{1,7},{2,0},{3,1},{4,2},{5,3},{6,4},{7,5},{8,14},{9,15},{10,... | collective-permute-start | bytes 3145736 | tf_op jit(solution)/shard_map/ppermute | solution.py:43
  15.4 13.3 %collective-permute-start.3 = (bf16[1,2,256,512]{3,2,1,0:T(8,128)(2,1)S(1)}, bf16[1,2,256,512]{3,2,1,0:T(8,128)(2,1)}, u32[]{:S(2)}, u32[]{:S(2)}) collective-permute-start(bf16[1,2,256,512]{3,2,1,0:T(8,128)(2,1)S(1)} %get-tuple-element.42), channel_id=1, source_target_pairs={{0,65},{1,64},{2,67},{3,66},{4,69},{5,68},{6,71},{7,70},{8,73},{9,... | collective-permute-start | bytes 1572872 | tf_op jit(solution)/shard_map/ppermute | solution.py:43
  15.9 13.1 %collective-permute-start.2 = (bf16[1,2,256,512]{3,2,1,0:T(8,128)(2,1)S(1)}, bf16[1,2,256,512]{3,2,1,0:T(8,128)(2,1)}, u32[]{:S(2)}, u32[]{:S(2)}) collective-permute-start(bf16[1,2,256,512]{3,2,1,0:T(8,128)(2,1)S(1)} %get-tuple-element.43.refs_8_), channel_id=1, source_target_pairs={{0,64},{1,65},{2,66},{3,67},{4,68},{5,69},{6,70},{7,71},{8,72},{9,... | collective-permute-start | bytes 1572872 | tf_op jit(solution)/shard_map/ppermute | solution.py:43
  38.2 3.3 %copy-start.8 = (bf16[2,2,256,512]{3,2,1,0:T(8,128)(2,1)}, bf16[2,2,256,512]{3,2,1,0:T(8,128)(2,1)S(1)}, u32[]{:S(2)}) copy-start(bf16[2,2,256,512]{3,2,1,0:T(8,128)(2,1)S(1)} %collective-permute-done.refs_9_) | copy-start | bytes 3145732
  38.4 24.5 %collective-permute-start.4 = (bf16[2,2,256,512]{3,2,1,0:T(8,128)(2,1)}, bf16[2,2,256,512]{3,2,1,0:T(8,128)(2,1)}, u32[]{:S(2)}, u32[]{:S(2)}) collective-permute-start(bf16[2,2,256,512]{3,2,1,0:T(8,128)(2,1)} %pad_maximum_fusion.4), channel_id=1, source_target_pairs={{0,6},{1,7},{2,0},{3,1},{4,2},{5,3},{6,4},{7,5},{8,14},{9,15},{10,... | collective-permute-start | bytes 3145736 | tf_op jit(solution)/shard_map/ppermute | solution.py:43
  42.6 23.7 %collective-permute-start.5 = (bf16[2,2,256,512]{3,2,1,0:T(8,128)(2,1)}, bf16[2,2,256,512]{3,2,1,0:T(8,128)(2,1)S(1)}, u32[]{:S(2)}, u32[]{:S(2)}) collective-permute-start(bf16[2,2,256,512]{3,2,1,0:T(8,128)(2,1)} %pad_maximum_fusion.5), channel_id=1, source_target_pairs={{0,64},{1,65},{2,66},{3,67},{4,68},{5,69},{6,70},{7,71},{8,72},{9,... | collective-permute-start | bytes 3145736 | tf_op jit(solution)/shard_map/ppermute | solution.py:43
  43.8 25.3 %copy-start.16 = (f32[512]{0:T(512)S(1)}, f32[512]{0:T(512)}, u32[]{:S(2)}) copy-start(f32[512]{0:T(512)} %param.10) | copy-start | bytes 6148
  43.8 26.1 %copy-start.17 = (s32[2,2]{1,0:T(2,128)S(1)}, s32[2,2]{1,0:T(2,128)}, u32[]{:S(2)}) copy-start(s32[2,2]{1,0:T(2,128)} %param.12) | copy-start | bytes 52
  43.8 26.1 %copy-start.18 = (s32[2,2]{1,0:T(2,128)S(1)}, s32[2,2]{1,0:T(2,128)}, u32[]{:S(2)}) copy-start(s32[2,2]{1,0:T(2,128)} %param.11) | copy-start | bytes 52
  43.8 26.8 %copy-start.19 = (s32[4]{0:T(128)S(1)}, s32[4]{0:T(128)}, u32[]{:S(2)}) copy-start(s32[4]{0:T(128)} %constant.166) | copy-start | bytes 52
  44.9 29.8 %collective-permute-start.7 = (bf16[2,2,256,512]{3,2,1,0:T(8,128)(2,1)}, bf16[2,2,256,512]{3,2,1,0:T(8,128)(2,1)S(1)}, u32[]{:S(2)}, u32[]{:S(2)}) collective-permute-start(bf16[2,2,256,512]{3,2,1,0:T(8,128)(2,1)} %pad_maximum_fusion.6), channel_id=1, source_target_pairs={{0,65},{1,64},{2,67},{3,66},{4,69},{5,68},{6,71},{7,70},{8,73},{9,... | collective-permute-start | bytes 3145736 | tf_op jit(solution)/shard_map/ppermute | solution.py:43
  45.2 27.8 %collective-permute-start.8 = (bf16[1,2,256,512]{3,2,1,0:T(8,128)(2,1)}, bf16[1,2,256,512]{3,2,1,0:T(8,128)(2,1)}, u32[]{:S(2)}, u32[]{:S(2)}) collective-permute-start(bf16[1,2,256,512]{3,2,1,0:T(8,128)(2,1)} %get-tuple-element.23), channel_id=1, source_target_pairs={{0,8},{2,2},{4,4},{6,6},{8,16},{10,10},{12,12},{14,14},{16,24},{18... | collective-permute-start | bytes 1572872 | tf_op jit(solution)/shard_map/ppermute | solution.py:43
  46.6 28.1 %collective-permute-start.9 = (bf16[1,2,256,512]{3,2,1,0:T(8,128)(2,1)}, bf16[1,2,256,512]{3,2,1,0:T(8,128)(2,1)}, u32[]{:S(2)}, u32[]{:S(2)}) collective-permute-start(bf16[1,2,256,512]{3,2,1,0:T(8,128)(2,1)} %get-tuple-element.24), channel_id=1, source_target_pairs={{0,2},{2,4},{4,6},{6,8},{8,10},{10,12},{12,14},{14,16},{16,18},{18... | collective-permute-start | bytes 1572872 | tf_op jit(solution)/shard_map/ppermute | solution.py:43
  62.9 11.8 %collective-permute-start.10 = (bf16[1,2,256,512]{3,2,1,0:T(8,128)(2,1)}, bf16[1,2,256,512]{3,2,1,0:T(8,128)(2,1)}, u32[]{:S(2)}, u32[]{:S(2)}) collective-permute-start(bf16[1,2,256,512]{3,2,1,0:T(8,128)(2,1)} %get-tuple-element.25), channel_id=1, source_target_pairs={{0,4},{2,6},{4,8},{6,2},{8,12},{10,14},{12,16},{14,10},{16,20},{18... | collective-permute-start | bytes 1572872 | tf_op jit(solution)/shard_map/ppermute | solution.py:43
  66.3 6.7 %copy-start.4 = (bf16[2,2,256,512]{3,2,1,0:T(8,128)(2,1)}, bf16[2,2,256,512]{3,2,1,0:T(8,128)(2,1)S(1)}, u32[]{:S(2)}) copy-start(bf16[2,2,256,512]{3,2,1,0:T(8,128)(2,1)S(1)} %collective-permute-done.5.refs_8_.refs_9_) | copy-start | bytes 3145732
  66.3 8.4 %collective-permute-start.11 = (bf16[1,2,256,512]{3,2,1,0:T(8,128)(2,1)}, bf16[1,2,256,512]{3,2,1,0:T(8,128)(2,1)}, u32[]{:S(2)}, u32[]{:S(2)}) collective-permute-start(bf16[1,2,256,512]{3,2,1,0:T(8,128)(2,1)} %get-tuple-element.26), channel_id=1, source_target_pairs={{0,6},{2,8},{4,2},{6,4},{8,14},{10,16},{12,10},{14,12},{16,22},{18... | collective-permute-start | bytes 1572872 | tf_op jit(solution)/shard_map/ppermute | solution.py:43
  73.0 37.5 %collective-permute-start.6 = (bf16[2,2,256,512]{3,2,1,0:T(8,128)(2,1)}, bf16[2,2,256,512]{3,2,1,0:T(8,128)(2,1)}, u32[]{:S(2)}, u32[]{:S(2)}) collective-permute-start(bf16[2,2,256,512]{3,2,1,0:T(8,128)(2,1)} %collective-permute-done.4), channel_id=1, source_target_pairs={{0,6},{1,7},{2,0},{3,1},{4,2},{5,3},{6,4},{7,5},{8,14},{9,15},{10,... | collective-permute-start | bytes 3145736 | tf_op jit(solution)/shard_map/ppermute | solution.py:43
  78.0 37.7 %collective-permute-start.12 = (bf16[3,2,256,512]{3,2,1,0:T(8,128)(2,1)}, bf16[3,2,256,512]{3,2,1,0:T(8,128)(2,1)S(1)}, u32[]{:S(2)}, u32[]{:S(2)}) collective-permute-start(bf16[3,2,256,512]{3,2,1,0:T(8,128)(2,1)} %pad_maximum_fusion), channel_id=1, source_target_pairs={{0,64},{1,65},{2,66},{3,67},{4,68},{5,69},{6,70},{7,71},{8,72},{9,... | collective-permute-start | bytes 4718600 | tf_op jit(solution)/shard_map/ppermute | solution.py:43
  79.2 49.6 %collective-permute-start.13 = (bf16[3,2,256,512]{3,2,1,0:T(8,128)(2,1)}, bf16[3,2,256,512]{3,2,1,0:T(8,128)(2,1)S(1)}, u32[]{:S(2)}, u32[]{:S(2)}) collective-permute-start(bf16[3,2,256,512]{3,2,1,0:T(8,128)(2,1)} %pad_maximum_fusion.1), channel_id=1, source_target_pairs={{0,65},{1,66},{2,67},{3,68},{4,69},{5,70},{6,71},{7,72},{8,73},{9,... | collective-permute-start | bytes 4718600 | tf_op jit(solution)/shard_map/ppermute | solution.py:43
  115.7 20.4 %copy-start.3 = (bf16[3,2,256,512]{3,2,1,0:T(8,128)(2,1)}, bf16[3,2,256,512]{3,2,1,0:T(8,128)(2,1)S(1)}, u32[]{:S(2)}) copy-start(bf16[3,2,256,512]{3,2,1,0:T(8,128)(2,1)S(1)} %collective-permute-done.12.refs_12_.refs_13_.refs_14_) | copy-start | bytes 4718596
  128.9 20.8 %copy-start.2 = (bf16[3,2,256,512]{3,2,1,0:T(8,128)(2,1)}, bf16[3,2,256,512]{3,2,1,0:T(8,128)(2,1)S(1)}, u32[]{:S(2)}) copy-start(bf16[3,2,256,512]{3,2,1,0:T(8,128)(2,1)S(1)} %collective-permute-done.13.refs_12_.refs_13_.refs_14_) | copy-start | bytes 4718596
  128.9 20.8 %collective-permute-start.14 = (bf16[1,2,256,512]{3,2,1,0:T(8,128)(2,1)}, bf16[1,2,256,512]{3,2,1,0:T(8,128)(2,1)}, u32[]{:S(2)}, u32[]{:S(2)}) collective-permute-start(bf16[1,2,256,512]{3,2,1,0:T(8,128)(2,1)} %get-tuple-element.30), channel_id=1, source_target_pairs={{0,65},{1,64},{2,67},{3,66},{4,69},{5,68},{6,71},{7,70},{8,73},{9,... | collective-permute-start | bytes 1572872 | tf_op jit(solution)/shard_map/ppermute | solution.py:43
  133.7 16.1 %collective-permute-start.16 = (bf16[1,2,256,512]{3,2,1,0:T(8,128)(2,1)}, bf16[1,2,256,512]{3,2,1,0:T(8,128)(2,1)S(1)}, u32[]{:S(2)}, u32[]{:S(2)}) collective-permute-start(bf16[1,2,256,512]{3,2,1,0:T(8,128)(2,1)} %get-tuple-element.31), channel_id=1, source_target_pairs={{0,64},{1,65},{2,66},{3,67},{4,68},{5,69},{6,70},{7,71},{8,72},{9,... | collective-permute-start | bytes 1572872 | tf_op jit(solution)/shard_map/ppermute | solution.py:43
  149.6 22.6 %collective-permute-start.15 = (bf16[1,2,256,512]{3,2,1,0:T(8,128)(2,1)}, bf16[1,2,256,512]{3,2,1,0:T(8,128)(2,1)S(1)}, u32[]{:S(2)}, u32[]{:S(2)}) collective-permute-start(bf16[1,2,256,512]{3,2,1,0:T(8,128)(2,1)} %collective-permute-done.14.refs_4_), channel_id=1, source_target_pairs={{0,64},{1,65},{2,66},{3,67},{4,68},{5,69},{6,70},{7,71},{8,72},{9,... | collective-permute-start | bytes 1572872 | tf_op jit(solution)/shard_map/ppermute | solution.py:43
  149.7 13.9 %copy-start.13 = (bf16[1,2,256,512]{3,2,1,0:T(8,128)(2,1)}, bf16[1,2,256,512]{3,2,1,0:T(8,128)(2,1)S(1)}, u32[]{:S(2)}) copy-start(bf16[1,2,256,512]{3,2,1,0:T(8,128)(2,1)S(1)} %collective-permute-done.16.refs_3_) | copy-start | bytes 1572868
  149.8 30.7 %collective-permute-start.17 = (bf16[1,2,256,512]{3,2,1,0:T(8,128)(2,1)S(1)}, bf16[1,2,256,512]{3,2,1,0:T(8,128)(2,1)S(1)}, u32[]{:S(2)}, u32[]{:S(2)}) collective-permute-start(bf16[1,2,256,512]{3,2,1,0:T(8,128)(2,1)S(1)} %collective-permute-done.16.refs_3_), channel_id=1, source_target_pairs={{0,65},{1,66},{2,67},{3,68},{4,69},{5,70},{6,71},{7,72},{8,73},{9,... | collective-permute-start | bytes 1572872 | tf_op jit(solution)/shard_map/ppermute | solution.py:43
  233.2 18.7 %all-to-all-start.1 = ((bf16[8,32,512]{2,1,0:T(8,128)(2,1)}), bf16[8,32,512]{2,1,0:T(8,128)(2,1)S(1)}, u32[]{:S(2)}, u32[]{:S(2)}) async-start(bf16[8,32,512]{2,1,0:T(8,128)(2,1)} %broadcast_in_dim.8), calls=%async_computation.1 | async-start | bytes 524288 | tf_op jit(solution)/shard_map/all_to_all | solution.py:198
  240.3 12.2 %copy-start.1 = (f32[256]{0:T(256)S(1)}, f32[256]{0:T(256)}, u32[]{:S(2)}) copy-start(f32[256]{0:T(256)} %param.9) | copy-start | bytes 3076
  (7 other events, 12.7 us)

commit v3 on v2

--- a/solution.py
+++ b/solution.py
@@ -23,18 +23,19 @@
     return l ^ 65
 
 
+def crossing(l):
+    return l & 63 == 63
+
+
 def onward_hop(l):
+    if crossing(l):
+        return (l + 1) % 128
     to = l ^ 65
     return to if to & 1 else (to + 2) % 128
 
 
-def before_hop(by):
-    def to(l):
-        y = (((l >> 1) & 3) + by) % 4
-        there = (l & ~6) | (y << 1)
-        return (there + 8) % 128 if y == 0 else there
-
-    return to
+def next_row(l):
+    return l if l & 1 else (l + 2) % 128
 
 
 def send(array, to, after=(), only=lambda l: True):
@@ -214,66 +215,67 @@
         there = (y + k) % 4 * 2
         return block(there + x_hi), block(there + 1 - x_hi)
 
+    order = jnp.array([0, 1, 3, 2], jnp.int32)
+    here = (y - order) % 4 * 2
+    own_ids = jnp.concatenate([here + x_hi, here + 1 - x_hi]).astype(jnp.int32)
+    shifted = (here + 6 * (1 - x_hi)) % 8
+    before_ids = jnp.concatenate([shifted + x_hi, shifted + 1 - x_hi]).astype(jnp.int32)
+
+    wide = jnp.float32
     same0, other0 = for_row(0)
     a0s = send(same0, same_hop)
     a0o = send(other0, other_hop)
     y1 = send(jnp.concatenate(for_row(1)), along_y(1))
     y3 = send(jnp.concatenate(for_row(3)), along_y(3))
-    third = jnp.concatenate(for_row(2))
-    even = lambda l: l & 1 == 0
-    block_ahead = {k: block(((y + k) % 4 * 2 + 7) % 8) for k in range(4)}
-    y1, y3, a0s, a0o, third, block_ahead = lax.optimization_barrier(
-        (y1, y3, a0s, a0o, third, block_ahead)
-    )
-    half = send(third, along_y(3))
+    y1, y3, a0s, a0o, third = lax.optimization_barrier(
+        (y1, y3, a0s, a0o, jnp.concatenate(for_row(2)))
+    )
+    crosses = (device & 63) == 63
+
+    def onward(mine, passing):
+        return send(jnp.where(crosses, mine, passing), onward_hop)
+
     same1 = jnp.concatenate([y1[:1], y3[:1]])
     other1 = jnp.concatenate([y1[1:], y3[1:]])
     a1s = send(same1, same_hop)
     a1o = send(other1, other_hop)
-    ahead = {k: send(block_ahead[k], before_hop(k), (), even) for k in range(4)}
-    y2 = send(half, along_y(3), (a1s,))
-    b1s = send(jnp.concatenate([a0o, a1o]), same_hop, (a1s, *ahead.values()))
-    b1o = send(jnp.concatenate([a0s, a1s]), onward_hop, (a1o, *ahead.values()))
-    a2s = send(y2[:1], same_hop, (b1s, b1o))
-    a2o = send(y2[1:], other_hop, (b1s, b1o))
-    b2s = send(a2o, same_hop)
-    b2o = send(a2s, onward_hop)
-
-    order = jnp.array([0, 1, 3, 2], jnp.int32)
-    here = (y - order) % 4 * 2
-    near_ids = here + x_hi
-    cross_ids = here + 1 - x_hi
-    late_ids = jnp.where(x_hi == 0, (here + 6) % 8 + 1, cross_ids)
-    own_ids = jnp.concatenate([near_ids, cross_ids]).astype(jnp.int32)
-    before_ids = jnp.concatenate([near_ids, late_ids]).astype(jnp.int32)
-
-    wide = jnp.float32
+    half = send(third, along_y(3))
+    b0s = send(a0o, same_hop)
+    b0o = onward(same0, a0s)
+    r1 = send(jnp.concatenate([other0, other1]), next_row)
+    a1s, a1o, half, b0s, b0o = lax.optimization_barrier((a1s, a1o, half, b0s, b0o))
+    y2 = send(half, along_y(3))
+    b1s = send(a1o, same_hop)
+    b1o = onward(same1, a1s)
     far = transform(
         metric,
         own_ids,
         [(a0s, 0, 0), (a1s, 0, 1), (a1s, 1, 2), (a0o, 0, 4), (a1o, 0, 5), (a1o, 1, 6)],
         dtype=wide,
     )
+    y2, b1s, b1o, r1, far = lax.optimization_barrier((y2, b1s, b1o, r1, far))
+    a2s = send(y2[:1], same_hop)
+    a2o = send(y2[1:], other_hop)
     own = transform(
         metric,
         own_ids,
-        [(same0, 0, 0), (y1, 0, 1), (y3, 0, 2), (y2, 0, 3), (b1s, 0, 4), (b1s, 1, 5), (b1s, 2, 6)],
+        [(same0, 0, 0), (y1, 0, 1), (y3, 0, 2), (y2, 0, 3), (b0s, 0, 4), (b1s, 0, 5), (b1s, 1, 6)],
         dtype=wide,
     )
-    near = jnp.where(
-        x_hi == 0,
-        jnp.concatenate([ahead[0], ahead[1], ahead[3], ahead[2]]),
-        jnp.concatenate([other0, other1, y2[1:]]),
-    )
+    a2s, a2o, own = lax.optimization_barrier((a2s, a2o, own))
+    r2 = send(y2[1:], next_row)
+    b2s = send(a2o, same_hop)
+    b2o = onward(y2[:1], a2s)
+
     before = transform(
         metric,
         before_ids,
-        [(near, k, k) for k in range(4)] + [(b1o, k, 4 + k) for k in range(3)],
+        [(r1, 0, 0), (r1, 1, 1), (r1, 2, 2), (b0o, 0, 4), (b1o, 0, 5), (b1o, 1, 6)],
         dtype=wide,
     )
     far = transform(metric, own_ids, [(a2s, 0, 3), (a2o, 0, 7)], far)
     own = transform(metric, own_ids, [(b2s, 0, 7)], own)
-    before = transform(metric, before_ids, [(b2o, 0, 7)], before)
+    before = transform(metric, before_ids, [(r2, 0, 3), (b2o, 0, 7)], before)
 
     ints = jnp.concatenate([partner, screen], axis=1).astype(jnp.int32)
     owners = jnp.stack([device, (device - 1) % 128, (device - 64) % 128])

time: 254 us -> 243 us (0.957)
  blocking collectives: 31.7 us -> 14.4 us
  waiting for transfers between devices: 50.4 us -> 56.2 us
    all_to_all x1, blocking collectives: 31.7 us -> 14.4 us  [summed_at_owner(): lax.all_to_all(pieces, 'occ', split_axis=0, concat_axis=0, tiled=True)]
    ppermute x18, starting transfers between devices: 43.5 us -> 36.9 us  [send(): lax.ppermute(array, AXES, [(l, to(l)) for l in range(128) if only(l)])]
    all_to_all x1, starting transfers between devices: 7.18 us -> 13.2 us  [summed_for_everyone(): arrived = lax.all_to_all(copies, 'aux', 0, 0, tiled=True)]
    ppermute x18, waiting for transfers between devices: 50.4 us -> 56.2 us  [send(): lax.ppermute(array, AXES, [(l, to(l)) for l in range(128) if only(l)])]
  transfers between devices with their start and end apart: 19 -> 19, of which waited for: 7 -> 8; matrix products, arithmetic and copies ran while one was open for 7% -> 7% of each run, Pallas kernels for 27% -> 27%
where the time goes in v3:
time: 243 us; the launch traced here: 242 us
  Pallas kernels  86.1 us (35%)
  waiting for transfers between devices  56.2 us (23%)
  starting transfers between devices  50.1 us (21%)
  local copies, waits for them, and re-layouts  18.7 us (8%)
  other arithmetic  15.7 us (6%)
  blocking collectives  14.4 us (6%)
    pallas_call x6, Pallas kernels, transform(): pl.pallas_call(lambda *refs: transform_kernel(count, *refs), out_shape=ja...  62.7 us
    ppermute x18, waiting for transfers between devices, send(): lax.ppermute(array, AXES, [(l, to(l)) for l in range(128) if only(l)])  56.2 us
    ppermute x18, starting transfers between devices, send(): lax.ppermute(array, AXES, [(l, to(l)) for l in range(128) if only(l)])  36.9 us
    all_to_all x1, blocking collectives, summed_at_owner(): lax.all_to_all(pieces, 'occ', split_axis=0, concat_axis=0, tiled=True)  14.4 us
    all_to_all x1, starting transfers between devices, summed_for_everyone(): arrived = lax.all_to_all(copies, 'aux', 0, 0, tiled=True)  13.2 us
    pallas_call x1, Pallas kernels, pairs(): pl.pallas_call(pair_kernel, out_shape=(jax.ShapeDtypeStruct((2, 2, nvir,...  11.9 us
    pallas_call x1, Pallas kernels, gradient_of(): pl.pallas_call(gradient_kernel, out_shape=jax.ShapeDtypeStruct((naux, 2,...  11.5 us
    transpose x1, local copies, waits for them, and re-layouts, on_device(): by_owner = jnp.transpose(integrals, (1, 0, 2)).reshape(8, 2, ROWS, nvir)  6.54 us
  transfers between devices with their start and end apart: 19, of which 8 were waited for; matrix products, arithmetic and copies ran while one was open for 7% of the time, Pallas kernels for 27%

profile of v3, /device:TPU:4, one launch (start us, length us, event | category | flops | bytes accessed | tf_op | source)
XLA Modules:
  0.0 242.1 jit_solution(12358112174081160407)
XLA Ops:
  0.8 6.5 %copy.12 = bf16[16,256,512]{2,1,0:T(8,128)(2,1)} copy(bf16[16,256,512]{2,0,1:T(8,128)(2,1)} %bitcast.11) | data formatting | bytes 8388608 | tf_op jit(solution)/shard_map/transpose | solution.py:209
  7.3 3.5 %constant_dynamic-slice_fusion.1 = (bf16[1,2,256,512]{3,2,1,0:T(8,128)(2,1)}, bf16[1,2,256,512]{3,2,1,0:T(8,128)(2,1)}, bf16[1,2,256,512]{3,2,1,0:T(8,128)(2,1)}...) fusion(bf16[8,2,256,512]{3,2,1,0:T(8,128)(2,1)} %bitcast.10, ...), kind=kLoop, calls=%fused_computation.19 | loop fusion | bytes 8388640 | tf_op jit(solution)/shard_map/jit(dynamic_index_in_dim)/dynamic_slice | solution.py:212
  12.0 3.0 %collective-permute-start.1 = (bf16[2,2,256,512]{3,2,1,0:T(8,128)(2,1)}, bf16[2,2,256,512]{3,2,1,0:T(8,128)(2,1)S(1)}, u32[]{:S(2)}, u32[]{:S(2)}) collective-permute-start(bf16[2,2,256,512]{3,2,1,0:T(8,128)(2,1)} %pad_maximum_fusion.2), channel_id=1, source_target_pairs={{0,6},{1,7},{2,0},{3,1},{4,2},{5,3},{6,4},{7,5},{8,14},{9,15},{10,... | collective-permute-start | bytes 3145736 | tf_op jit(solution)/shard_map/ppermute | solution.py:44
  17.3 2.3 pad_maximum_fusion.3
  19.6 9.8 %collective-permute-done.2.refs_7_ = bf16[1,2,256,512]{3,2,1,0:T(8,128)(2,1)S(1)} collective-permute-done((bf16[1,2,256,512]{3,2,1,0:T(8,128)(2,1)S(1)}, bf16[1,2,256,512]{3,2,1,0:T(8,128)(2,1)S(1)}, u32[]{:S(2)}, u32[]{:S(2)}) %collective-permute-start.2) | collective-permute-done | bytes 524320 | tf_op jit(solution)/shard_map/ppermute | solution.py:44
  30.6 7.1 %collective-permute-done.1.refs_10_ = bf16[2,2,256,512]{3,2,1,0:T(8,128)(2,1)S(1)} collective-permute-done((bf16[2,2,256,512]{3,2,1,0:T(8,128)(2,1)}, bf16[2,2,256,512]{3,2,1,0:T(8,128)(2,1)S(1)}, u32[]{:S(2)}, u32[]{:S(2)}) %collective-permute-start.1) | collective-permute-done | bytes 1048608 | tf_op jit(solution)/shard_map/ppermute | solution.py:44
  37.7 4.4 %collective-permute-done.refs_9_ = bf16[2,2,256,512]{3,2,1,0:T(8,128)(2,1)S(1)} collective-permute-done((bf16[2,2,256,512]{3,2,1,0:T(8,128)(2,1)}, bf16[2,2,256,512]{3,2,1,0:T(8,128)(2,1)S(1)}, u32[]{:S(2)}, u32[]{:S(2)}) %collective-permute-start) | collective-permute-done | bytes 1048608 | tf_op jit(solution)/shard_map/ppermute | solution.py:44
  43.2 1.7 fusion.5
  46.2 2.0 collective-permute-start.5
  49.2 2.4 collective-permute-start.4
  54.2 2.7 %pad_maximum_fusion = bf16[3,2,256,512]{3,2,1,0:T(8,128)(2,1)} fusion(bf16[1,2,256,512]{3,2,1,0:T(8,128)(2,1)} %copy-done.7, bf16[1,2,256,512]{3,2,1,0:T(8,128)(2,1)} %copy-done.6, bf16[1,2,256,512]{3,2,1,0:T(8,128)(2,1)} %get-tuple-element.47), kind=kLoop, calls=%fused_computation.1 | loop fusion | flops 1572864 | bytes 3145728 | tf_op jit(solution)/shard_map/concatenate | solution.py:245
  56.9 1.5 collective-permute-done.8.refs_10_
  58.4 2.1 collective-permute-start.12
  61.0 23.6 %collective-permute-done.7.refs_12_ = bf16[1,2,256,512]{3,2,1,0:T(8,128)(2,1)} collective-permute-done((bf16[1,2,256,512]{3,2,1,0:T(8,128)(2,1)}, bf16[1,2,256,512]{3,2,1,0:T(8,128)(2,1)}, u32[]{:S(2)}, u32[]{:S(2)}) %collective-permute-start.7) | collective-permute-done | bytes 524320 | tf_op jit(solution)/shard_map/ppermute | solution.py:44
  85.9 1.7 collective-permute-start.10
  87.6 1.7 collective-permute-start.9
  90.6 12.3 %transform.6.refs_5_ = f32[2,2048,512]{2,1,0:T(8,128)} custom-call(s32[8]{0:T(128)} %pad_add_fusion.1.refs_0_, bf16[2048,2048]{1,0:T(8,128)(2,1)} %refs_2_.9, bf16[2048,2048]{1,0:T(8,128)(2,1)} %refs_2_.9, bf16[2048,2048]{1,0:T(8,128)(2,1)} %refs_2_.9, bf16[2048,2048]{1,0:T(8,128)(2,1)} %refs_2_.9, bf16[2048,2048]{1,0:T(8,128)(2,1)} %refs_2_.9, ...), custom_call_target="tpu_custom_call" | custom-call | flops 6442450944 | bytes 17825792 | tf_op jit(solution)/shard_map/transform/pallas_call | solution.py:73
  102.9 5.8 %collective-permute-done.11.refs_11_.refs_12_ = bf16[2,2,256,512]{3,2,1,0:T(8,128)(2,1)} collective-permute-done((bf16[2,2,256,512]{3,2,1,0:T(8,128)(2,1)}, bf16[2,2,256,512]{3,2,1,0:T(8,128)(2,1)}, u32[]{:S(2)}, u32[]{:S(2)}) %collective-permute-start.11) | collective-permute-done | bytes 1048608 | tf_op jit(solution)/shard_map/ppermute | solution.py:44
  108.7 2.8 %collective-permute-done.9.refs_11_ = bf16[2,2,256,512]{3,2,1,0:T(8,128)(2,1)S(1)} collective-permute-done((bf16[2,2,256,512]{3,2,1,0:T(8,128)(2,1)}, bf16[2,2,256,512]{3,2,1,0:T(8,128)(2,1)S(1)}, u32[]{:S(2)}, u32[]{:S(2)}) %collective-permute-start.9) | collective-permute-done | bytes 1048608 | tf_op jit(solution)/shard_map/ppermute | solution.py:44
  112.7 17.6 %collective-permute-start.14 = (bf16[1,2,256,512]{3,2,1,0:T(8,128)(2,1)}, bf16[1,2,256,512]{3,2,1,0:T(8,128)(2,1)}, u32[]{:S(2)}, u32[]{:S(2)}) collective-permute-start(bf16[1,2,256,512]{3,2,1,0:T(8,128)(2,1)} %get-tuple-element.53), channel_id=1, source_target_pairs={{0,65},{1,64},{2,67},{3,66},{4,69},{5,68},{6,71},{7,70},{8,73},{9,... | collective-permute-start | bytes 1572872 | tf_op jit(solution)/shard_map/ppermute | solution.py:44
  130.3 1.7 collective-permute-start.16
  132.0 3.1 %collective-permute-start.13 = (bf16[1,2,256,512]{3,2,1,0:T(8,128)(2,1)}, bf16[1,2,256,512]{3,2,1,0:T(8,128)(2,1)S(1)}, u32[]{:S(2)}, u32[]{:S(2)}) collective-permute-start(bf16[1,2,256,512]{3,2,1,0:T(8,128)(2,1)} %get-tuple-element.54), channel_id=1, source_target_pairs={{0,64},{1,65},{2,66},{3,67},{4,68},{5,69},{6,70},{7,71},{8,72},{9,... | collective-permute-start | bytes 1572872 | tf_op jit(solution)/shard_map/ppermute | solution.py:44
  135.1 13.5 %transform.7.refs_3_ = f32[2,2048,512]{2,1,0:T(8,128)} custom-call(s32[8]{0:T(128)} %pad_add_fusion.1.refs_0_, bf16[2048,2048]{1,0:T(8,128)(2,1)} %refs_2_.9, bf16[2048,2048]{1,0:T(8,128)(2,1)} %refs_2_.9, bf16[2048,2048]{1,0:T(8,128)(2,1)} %refs_2_.9, bf16[2048,2048]{1,0:T(8,128)(2,1)} %refs_2_.9, bf16[2048,2048]{1,0:T(8,128)(2,1)} %refs_2_.9, ...), custom_call_target="tpu_custom_call" | custom-call | flops 7516192768 | bytes 19398656 | tf_op jit(solution)/shard_map/transform/pallas_call | solution.py:73
  148.6 1.3 broadcast_select_fusion.1
  150.3 12.4 %transform.9.refs_5_ = f32[2,2048,512]{2,1,0:T(8,128)} custom-call(s32[8]{0:T(128)} %pad_add_fusion.2.refs_0_, bf16[2048,2048]{1,0:T(8,128)(2,1)} %refs_2_.9, bf16[2048,2048]{1,0:T(8,128)(2,1)} %refs_2_.9, bf16[2048,2048]{1,0:T(8,128)(2,1)} %refs_2_.9, bf16[2048,2048]{1,0:T(8,128)(2,1)} %refs_2_.9, bf16[2048,2048]{1,0:T(8,128)(2,1)} %refs_2_.9, ...), custom_call_target="tpu_custom_call" | custom-call | flops 6442450944 | bytes 17825792 | tf_op jit(solution)/shard_map/transform/pallas_call | solution.py:73
  162.7 8.5 %transform.11.far = bf16[2,2048,512]{2,1,0:T(8,128)(2,1)} custom-call(s32[8]{0:T(128)} %pad_add_fusion.1.refs_0_, bf16[2048,2048]{1,0:T(8,128)(2,1)} %refs_2_.9, bf16[2048,2048]{1,0:T(8,128)(2,1)} %refs_2_.9, bf16[1,2,256,512]{3,2,1,0:T(8,128)(2,1)} %copy-done.11, bf16[1,2,256,512]{3,2,1,0:T(8,128)(2,1)} %collective-permute-done.14.refs_4_, ...), custom_call_target="tpu_custom_call" | custom-call | flops 2147483648 | bytes 15728640 | tf_op jit(solution)/shard_map/transform/pallas_call | solution.py:73
  172.0 7.5 %transform.8.left = bf16[2,2048,512]{2,1,0:T(8,128)(2,1)} custom-call(s32[8]{0:T(128)} %pad_add_fusion.1.refs_0_, bf16[2048,2048]{1,0:T(8,128)(2,1)} %refs_2_.9, bf16[1,2,256,512]{3,2,1,0:T(8,128)(2,1)} %copy-done.14, f32[2,2048,512]{2,1,0:T(8,128)} %transform.7.refs_3_), custom_call_target="tpu_custom_call" | custom-call | flops 1073741824 | bytes 14155776 | tf_op jit(solution)/shard_map/transform/pallas_call | solution.py:73
  181.1 8.5 %transform.10.before = bf16[2,2048,512]{2,1,0:T(8,128)(2,1)} custom-call(s32[8]{0:T(128)} %pad_add_fusion.2.refs_0_, bf16[2048,2048]{1,0:T(8,128)(2,1)} %refs_2_.9, bf16[2048,2048]{1,0:T(8,128)(2,1)} %refs_2_.9, bf16[1,2,256,512]{3,2,1,0:T(8,128)(2,1)} %copy-done.12, bf16[1,2,256,512]{3,2,1,0:T(8,128)(2,1)} %copy-done.13, f32[2,2048,512]{2,1,0:T(8,128)} %transform.9.refs_5_), custom_call_target="tpu_custom_call" | custom-call | flops 2147483648 | bytes 15728640 | tf_op jit(solution)/shard_map/transform/pallas_call | solution.py:73
  189.6 11.9 %pairs.1 = (bf16[2,2,512,512]{3,2,1,0:T(8,128)(2,1)}, bf16[512,512]{1,0:T(8,128)(2,1)}) custom-call(s32[2,4]{1,0:T(2,128)} %pad_add_fusion.ints, f32[3,2]{1,0:T(4,128)} %reshape.79.floats, bf16[2,2048,512]{2,1,0:T(8,128)(2,1)} %transform.8.left, bf16[2,2048,512]{2,1,0:T(8,128)(2,1)} %transform.10.before, bf16[2,2048,512]{2,1,0:T(8,128)(2,1)} %transform.11.far, ...), custom_call_target="tpu_custom_call" | custom-call | flops 5368709120 | bytes 12582912 | tf_op jit(solution)/shard_map/pairs/pallas_call | solution.py:124
  201.5 14.4 %all_to_all.10 = bf16[16,32,512]{2,1,0:T(8,128)(2,1)S(1)} all-to-all(bf16[16,32,512]{2,1,0:T(8,128)(2,1)} %bitcast.12), channel_id=1, replica_groups=mesh['occ'=16,'aux'=8] {'occ'}, dimensions={0} | all-to-all | bytes 1048576 | tf_op jit(solution)/shard_map/all_to_all | solution.py:193
  216.7 13.2 %all-to-all-start.1 = ((bf16[8,32,512]{2,1,0:T(8,128)(2,1)}), bf16[8,32,512]{2,1,0:T(8,128)(2,1)S(1)}, u32[]{:S(2)}, u32[]{:S(2)}) async-start(bf16[8,32,512]{2,1,0:T(8,128)(2,1)} %broadcast_in_dim.8), calls=%async_computation.1 | async-start | bytes 524288 | tf_op jit(solution)/shard_map/all_to_all | solution.py:199
  229.9 11.5 %gradient.1 = bf16[2048,2,512]{2,1,0:T(2,128)(2,1)} custom-call(s32[2,4]{1,0:T(2,128)} %pad_add_fusion.ints, bf16[2,2,512,512]{3,2,1,0:T(8,128)(2,1)} %get-tuple-element.40.amps, bf16[2,2048,512]{2,1,0:T(8,128)(2,1)} %transform.10.before, bf16[2,2048,512]{2,1,0:T(8,128)(2,1)} %transform.11.far), custom_call_target="tpu_custom_call" | custom-call | flops 4294967296 | bytes 12582912 | tf_op jit(solution)/shard_map/gradient/pallas_call | solution.py:172
  (83 shorter events, 19.2 us)
Async XLA Ops:
  0.6 51.3 %copy-start = (f32[256]{0:T(256)S(1)}, f32[256]{0:T(256)}, u32[]{:S(2)}) copy-start(f32[256]{0:T(256)} %param.9) | copy-start | bytes 3076
  10.8 34.1 %copy-start.5 = (bf16[1,2,256,512]{3,2,1,0:T(8,128)(2,1)}, bf16[1,2,256,512]{3,2,1,0:T(8,128)(2,1)S(1)}, u32[]{:S(2)}) copy-start(bf16[1,2,256,512]{3,2,1,0:T(8,128)(2,1)S(1)} %get-tuple-element.48.refs_8_) | copy-start | bytes 1572868
  12.0 25.7 %collective-permute-start.1 = (bf16[2,2,256,512]{3,2,1,0:T(8,128)(2,1)}, bf16[2,2,256,512]{3,2,1,0:T(8,128)(2,1)S(1)}, u32[]{:S(2)}, u32[]{:S(2)}) collective-permute-start(bf16[2,2,256,512]{3,2,1,0:T(8,128)(2,1)} %pad_maximum_fusion.2), channel_id=1, source_target_pairs={{0,6},{1,7},{2,0},{3,1},{4,2},{5,3},{6,4},{7,5},{8,14},{9,15},{10,... | collective-permute-start | bytes 3145736 | tf_op jit(solution)/shard_map/ppermute | solution.py:44
  16.0 26.0 %collective-permute-start = (bf16[2,2,256,512]{3,2,1,0:T(8,128)(2,1)}, bf16[2,2,256,512]{3,2,1,0:T(8,128)(2,1)S(1)}, u32[]{:S(2)}, u32[]{:S(2)}) collective-permute-start(bf16[2,2,256,512]{3,2,1,0:T(8,128)(2,1)} %pad_maximum_fusion.1), channel_id=1, source_target_pairs={{0,2},{1,3},{2,4},{3,5},{4,6},{5,7},{6,0},{7,1},{8,10},{9,11},{10,... | collective-permute-start | bytes 3145736 | tf_op jit(solution)/shard_map/ppermute | solution.py:44
  16.0 13.4 %collective-permute-start.2 = (bf16[1,2,256,512]{3,2,1,0:T(8,128)(2,1)S(1)}, bf16[1,2,256,512]{3,2,1,0:T(8,128)(2,1)S(1)}, u32[]{:S(2)}, u32[]{:S(2)}) collective-permute-start(bf16[1,2,256,512]{3,2,1,0:T(8,128)(2,1)S(1)} %get-tuple-element.48.refs_8_), channel_id=1, source_target_pairs={{0,64},{1,65},{2,66},{3,67},{4,68},{5,69},{6,70},{7,71},{8,72},{9,... | collective-permute-start | bytes 1572872 | tf_op jit(solution)/shard_map/ppermute | solution.py:44
  17.2 13.4 %collective-permute-start.3 = (bf16[1,2,256,512]{3,2,1,0:T(8,128)(2,1)}, bf16[1,2,256,512]{3,2,1,0:T(8,128)(2,1)}, u32[]{:S(2)}, u32[]{:S(2)}) collective-permute-start(bf16[1,2,256,512]{3,2,1,0:T(8,128)(2,1)} %get-tuple-element.47), channel_id=1, source_target_pairs={{0,65},{1,64},{2,67},{3,66},{4,69},{5,68},{6,71},{7,70},{8,73},{9,... | collective-permute-start | bytes 1572872 | tf_op jit(solution)/shard_map/ppermute | solution.py:44
  29.4 13.6 %copy-start.10 = (bf16[1,2,256,512]{3,2,1,0:T(8,128)(2,1)}, bf16[1,2,256,512]{3,2,1,0:T(8,128)(2,1)S(1)}, u32[]{:S(2)}) copy-start(bf16[1,2,256,512]{3,2,1,0:T(8,128)(2,1)S(1)} %collective-permute-done.2.refs_7_) | copy-start | bytes 1572868
  37.7 5.3 %copy-start.8 = (bf16[2,2,256,512]{3,2,1,0:T(8,128)(2,1)}, bf16[2,2,256,512]{3,2,1,0:T(8,128)(2,1)S(1)}, u32[]{:S(2)}) copy-start(bf16[2,2,256,512]{3,2,1,0:T(8,128)(2,1)S(1)} %collective-permute-done.1.refs_10_) | copy-start | bytes 3145732
  43.2 8.6 %copy-start.18 = (s32[4]{0:T(128)S(1)}, s32[4]{0:T(128)}, u32[]{:S(2)}) copy-start(s32[4]{0:T(128)} %constant.134) | copy-start | bytes 52
  43.2 15.2 %collective-permute-start.8 = (bf16[1,2,256,512]{3,2,1,0:T(8,128)(2,1)}, bf16[1,2,256,512]{3,2,1,0:T(8,128)(2,1)}, u32[]{:S(2)}, u32[]{:S(2)}) collective-permute-start(bf16[1,2,256,512]{3,2,1,0:T(8,128)(2,1)} %broadcast_select_fusion.2), channel_id=1, source_target_pairs={{0,65},{1,66},{2,67},{3,68},{4,69},{5,70},{6,71},{7,72},{8,73},{9,... | collective-permute-start | bytes 1572872 | tf_op jit(solution)/shard_map/ppermute | solution.py:44
  45.0 8.3 %copy-start.15 = (f32[512]{0:T(512)S(1)}, f32[512]{0:T(512)}, u32[]{:S(2)}) copy-start(f32[512]{0:T(512)} %param.10) | copy-start | bytes 6148
  46.2 38.5 %collective-permute-start.5 = (bf16[2,2,256,512]{3,2,1,0:T(8,128)(2,1)}, bf16[2,2,256,512]{3,2,1,0:T(8,128)(2,1)}, u32[]{:S(2)}, u32[]{:S(2)}) collective-permute-start(bf16[2,2,256,512]{3,2,1,0:T(8,128)(2,1)} %pad_maximum_fusion.5), channel_id=1, source_target_pairs={{0,65},{1,64},{2,67},{3,66},{4,69},{5,68},{6,71},{7,70},{8,73},{9,... | collective-permute-start | bytes 3145736 | tf_op jit(solution)/shard_map/ppermute | solution.py:44
  49.2 35.4 %collective-permute-start.4 = (bf16[2,2,256,512]{3,2,1,0:T(8,128)(2,1)}, bf16[2,2,256,512]{3,2,1,0:T(8,128)(2,1)S(1)}, u32[]{:S(2)}, u32[]{:S(2)}) collective-permute-start(bf16[2,2,256,512]{3,2,1,0:T(8,128)(2,1)} %pad_maximum_fusion.4), channel_id=1, source_target_pairs={{0,64},{1,65},{2,66},{3,67},{4,68},{5,69},{6,70},{7,71},{8,72},{9,... | collective-permute-start | bytes 3145736 | tf_op jit(solution)/shard_map/ppermute | solution.py:44
  51.7 33.0 %collective-permute-start.6 = (bf16[2,2,256,512]{3,2,1,0:T(8,128)(2,1)}, bf16[2,2,256,512]{3,2,1,0:T(8,128)(2,1)}, u32[]{:S(2)}, u32[]{:S(2)}) collective-permute-start(bf16[2,2,256,512]{3,2,1,0:T(8,128)(2,1)} %pad_maximum_fusion.3), channel_id=1, source_target_pairs={{0,6},{1,7},{2,0},{3,1},{4,2},{5,3},{6,4},{7,5},{8,14},{9,15},{10,... | collective-permute-start | bytes 3145736 | tf_op jit(solution)/shard_map/ppermute | solution.py:44
  51.8 32.8 %collective-permute-start.7 = (bf16[1,2,256,512]{3,2,1,0:T(8,128)(2,1)}, bf16[1,2,256,512]{3,2,1,0:T(8,128)(2,1)}, u32[]{:S(2)}, u32[]{:S(2)}) collective-permute-start(bf16[1,2,256,512]{3,2,1,0:T(8,128)(2,1)} %collective-permute-done.3.refs_10_), channel_id=1, source_target_pairs={{0,64},{1,65},{2,66},{3,67},{4,68},{5,69},{6,70},{7,71},{8,72},{9,... | collective-permute-start | bytes 1572872 | tf_op jit(solution)/shard_map/ppermute | solution.py:44
  52.0 37.9 %copy-start.16 = (s32[2,2]{1,0:T(2,128)S(1)}, s32[2,2]{1,0:T(2,128)}, u32[]{:S(2)}) copy-start(s32[2,2]{1,0:T(2,128)} %param.12) | copy-start | bytes 52
  52.0 37.9 %copy-start.17 = (s32[2,2]{1,0:T(2,128)S(1)}, s32[2,2]{1,0:T(2,128)}, u32[]{:S(2)}) copy-start(s32[2,2]{1,0:T(2,128)} %param.11) | copy-start | bytes 52
  58.4 44.5 %collective-permute-start.12 = (bf16[3,2,256,512]{3,2,1,0:T(8,128)(2,1)}, bf16[3,2,256,512]{3,2,1,0:T(8,128)(2,1)S(1)}, u32[]{:S(2)}, u32[]{:S(2)}) collective-permute-start(bf16[3,2,256,512]{3,2,1,0:T(8,128)(2,1)} %pad_maximum_fusion), channel_id=1, source_target_pairs={{0,2},{1,1},{2,4},{3,3},{4,6},{5,5},{6,8},{7,7},{8,10},{9,9},{10,1... | collective-permute-start | bytes 4718600 | tf_op jit(solution)/shard_map/ppermute | solution.py:44
  84.6 5.9 %copy-start.3 = (bf16[2,2,256,512]{3,2,1,0:T(8,128)(2,1)}, bf16[2,2,256,512]{3,2,1,0:T(8,128)(2,1)S(1)}, u32[]{:S(2)}) copy-start(bf16[2,2,256,512]{3,2,1,0:T(8,128)(2,1)S(1)} %collective-permute-done.4.refs_8_.refs_9_) | copy-start | bytes 3145732
  85.9 22.8 %collective-permute-start.11 = (bf16[2,2,256,512]{3,2,1,0:T(8,128)(2,1)}, bf16[2,2,256,512]{3,2,1,0:T(8,128)(2,1)}, u32[]{:S(2)}, u32[]{:S(2)}) collective-permute-start(bf16[2,2,256,512]{3,2,1,0:T(8,128)(2,1)} %broadcast_select_fusion), channel_id=1, source_target_pairs={{0,65},{1,66},{2,67},{3,68},{4,69},{5,70},{6,71},{7,72},{8,73},{9,... | collective-permute-start | bytes 3145736 | tf_op jit(solution)/shard_map/ppermute | solution.py:44
  85.9 22.8 %collective-permute-start.10 = (bf16[2,2,256,512]{3,2,1,0:T(8,128)(2,1)}, bf16[2,2,256,512]{3,2,1,0:T(8,128)(2,1)}, u32[]{:S(2)}, u32[]{:S(2)}) collective-permute-start(bf16[2,2,256,512]{3,2,1,0:T(8,128)(2,1)} %collective-permute-done.5.refs_11_.refs_12_), channel_id=1, source_target_pairs={{0,64},{1,65},{2,66},{3,67},{4,68},{5,69},{6,70},{7,71},{8,72},{9,... | collective-permute-start | bytes 3145736 | tf_op jit(solution)/shard_map/ppermute | solution.py:44
  87.6 23.9 %collective-permute-start.9 = (bf16[2,2,256,512]{3,2,1,0:T(8,128)(2,1)}, bf16[2,2,256,512]{3,2,1,0:T(8,128)(2,1)S(1)}, u32[]{:S(2)}, u32[]{:S(2)}) collective-permute-start(bf16[2,2,256,512]{3,2,1,0:T(8,128)(2,1)} %collective-permute-done.6), channel_id=1, source_target_pairs={{0,6},{1,7},{2,0},{3,1},{4,2},{5,3},{6,4},{7,5},{8,14},{9,15},{10,... | collective-permute-start | bytes 3145736 | tf_op jit(solution)/shard_map/ppermute | solution.py:44
  102.9 45.7 %copy-start.2 = (bf16[3,2,256,512]{3,2,1,0:T(8,128)(2,1)}, bf16[3,2,256,512]{3,2,1,0:T(8,128)(2,1)S(1)}, u32[]{:S(2)}) copy-start(bf16[3,2,256,512]{3,2,1,0:T(8,128)(2,1)S(1)} %collective-permute-done.12.refs_7_.refs_8_.refs_9_) | copy-start | bytes 4718596
  111.5 23.6 %copy-start.4 = (bf16[2,2,256,512]{3,2,1,0:T(8,128)(2,1)}, bf16[2,2,256,512]{3,2,1,0:T(8,128)(2,1)S(1)}, u32[]{:S(2)}) copy-start(bf16[2,2,256,512]{3,2,1,0:T(8,128)(2,1)S(1)} %collective-permute-done.9.refs_11_) | copy-start | bytes 3145732
  112.7 35.9 %collective-permute-start.14 = (bf16[1,2,256,512]{3,2,1,0:T(8,128)(2,1)}, bf16[1,2,256,512]{3,2,1,0:T(8,128)(2,1)}, u32[]{:S(2)}, u32[]{:S(2)}) collective-permute-start(bf16[1,2,256,512]{3,2,1,0:T(8,128)(2,1)} %get-tuple-element.53), channel_id=1, source_target_pairs={{0,65},{1,64},{2,67},{3,66},{4,69},{5,68},{6,71},{7,70},{8,73},{9,... | collective-permute-start | bytes 1572872 | tf_op jit(solution)/shard_map/ppermute | solution.py:44
  130.3 49.2 %collective-permute-start.16 = (bf16[1,2,256,512]{3,2,1,0:T(8,128)(2,1)}, bf16[1,2,256,512]{3,2,1,0:T(8,128)(2,1)S(1)}, u32[]{:S(2)}, u32[]{:S(2)}) collective-permute-start(bf16[1,2,256,512]{3,2,1,0:T(8,128)(2,1)} %get-tuple-element.53), channel_id=1, source_target_pairs={{0,2},{1,1},{2,4},{3,3},{4,6},{5,5},{6,8},{7,7},{8,10},{9,9},{10,1... | collective-permute-start | bytes 1572872 | tf_op jit(solution)/shard_map/ppermute | solution.py:44
  132.0 16.6 %collective-permute-start.13 = (bf16[1,2,256,512]{3,2,1,0:T(8,128)(2,1)}, bf16[1,2,256,512]{3,2,1,0:T(8,128)(2,1)S(1)}, u32[]{:S(2)}, u32[]{:S(2)}) collective-permute-start(bf16[1,2,256,512]{3,2,1,0:T(8,128)(2,1)} %get-tuple-element.54), channel_id=1, source_target_pairs={{0,64},{1,65},{2,66},{3,67},{4,68},{5,69},{6,70},{7,71},{8,72},{9,... | collective-permute-start | bytes 1572872 | tf_op jit(solution)/shard_map/ppermute | solution.py:44
  148.6 14.1 %copy-start.11 = (bf16[1,2,256,512]{3,2,1,0:T(8,128)(2,1)}, bf16[1,2,256,512]{3,2,1,0:T(8,128)(2,1)S(1)}, u32[]{:S(2)}) copy-start(bf16[1,2,256,512]{3,2,1,0:T(8,128)(2,1)S(1)} %collective-permute-done.13.refs_3_) | copy-start | bytes 1572868
  149.9 29.5 %collective-permute-start.17 = (bf16[1,2,256,512]{3,2,1,0:T(8,128)(2,1)S(1)}, bf16[1,2,256,512]{3,2,1,0:T(8,128)(2,1)S(1)}, u32[]{:S(2)}, u32[]{:S(2)}) collective-permute-start(bf16[1,2,256,512]{3,2,1,0:T(8,128)(2,1)S(1)} %broadcast_select_fusion.1), channel_id=1, source_target_pairs={{0,65},{1,66},{2,67},{3,68},{4,69},{5,70},{6,71},{7,72},{8,73},{9,... | collective-permute-start | bytes 1572872 | tf_op jit(solution)/shard_map/ppermute | solution.py:44
  150.2 21.0 %collective-permute-start.15 = (bf16[1,2,256,512]{3,2,1,0:T(8,128)(2,1)}, bf16[1,2,256,512]{3,2,1,0:T(8,128)(2,1)S(1)}, u32[]{:S(2)}, u32[]{:S(2)}) collective-permute-start(bf16[1,2,256,512]{3,2,1,0:T(8,128)(2,1)} %collective-permute-done.14.refs_4_), channel_id=1, source_target_pairs={{0,64},{1,65},{2,66},{3,67},{4,68},{5,69},{6,70},{7,71},{8,72},{9,... | collective-permute-start | bytes 1572872 | tf_op jit(solution)/shard_map/ppermute | solution.py:44
  216.7 24.7 %all-to-all-start.1 = ((bf16[8,32,512]{2,1,0:T(8,128)(2,1)}), bf16[8,32,512]{2,1,0:T(8,128)(2,1)S(1)}, u32[]{:S(2)}, u32[]{:S(2)}) async-start(bf16[8,32,512]{2,1,0:T(8,128)(2,1)} %broadcast_in_dim.8), calls=%async_computation.1 | async-start | bytes 524288 | tf_op jit(solution)/shard_map/all_to_all | solution.py:199
  229.9 12.2 %copy-start.1 = (f32[256]{0:T(256)S(1)}, f32[256]{0:T(256)}, u32[]{:S(2)}) copy-start(f32[256]{0:T(256)} %param.9) | copy-start | bytes 3076
  (6 other events, 10.0 us)

commit v4 on v3

--- a/solution.py
+++ b/solution.py
@@ -36,6 +36,17 @@
 
 def next_row(l):
     return l if l & 1 else (l + 2) % 128
+
+
+def to_row(by):
+    def to(l):
+        if l & 1:
+            return l
+        y = (((l >> 1) & 3) + by) % 4
+        there = (l & ~6) | (y << 1)
+        return (there + 8) % 128 if y == 0 else there
+
+    return to
 
 
 def send(array, to, after=(), only=lambda l: True):
@@ -90,69 +101,125 @@
     )
 
 
-def pair_kernel(ints, floats, left, before, far, row, column, amps, density, total):
-    slot = pl.program_id(0)
-    pair_sum = column[...] + row[...]
-
-    @pl.when(slot == 0)
+def finish_kernel(
+    ids,
+    ints,
+    floats,
+    m_far,
+    m_cross,
+    m_late,
+    own_sum,
+    before_sum,
+    far_sum,
+    b2s,
+    b2o,
+    a2s,
+    a2o,
+    row,
+    column,
+    amps,
+    density,
+    before,
+    far,
+    meet,
+):
+    step = pl.program_id(0)
+
+    @pl.when(step == 0)
     def _():
-        total[...] = jnp.zeros_like(total)
-
-    for rnd, rights in enumerate((before, far)):
-        local = ints[slot, rnd]
-        right = rights[local]
-        intersection = lax.dot_general(
-            left[0], right, (((0,), (0,)), ((), ())), preferred_element_type=jnp.float32
-        )
-        gap = pair_sum - floats[0, slot] - floats[1 + rnd, local]
-        kept = ints[slot, 2 + rnd].astype(jnp.float32)
-        amp = (kept * intersection / gap).astype(jnp.bfloat16)
-        amps[0, rnd] = amp
-        total[...] += lax.dot_general(
-            amp, amp, (((1,), (1,)), ((), ())), preferred_element_type=jnp.float32
-        )
-
-    @pl.when(slot == 1)
+        meet[...] = jnp.zeros_like(meet)
+
+    def closed(sofar, slot, *terms):
+        for metric, piece in terms:
+            sofar = sofar + jnp.dot(
+                metric[...], piece[0, slot], preferred_element_type=jnp.float32
+            )
+        return sofar.astype(jnp.bfloat16)
+
+    for slot in range(2):
+        before[slot] = closed(before_sum[slot], slot, (m_late, b2o))
+        far[slot] = closed(far_sum[slot], slot, (m_far, a2s), (m_cross, a2o))
+    for slot in range(2):
+        left = closed(own_sum[slot], slot, (m_cross, b2s)).T
+        for rnd, rights in enumerate((before, far)):
+            right = rights[ints[slot, rnd]]
+            meet[slot, rnd] += jnp.dot(left, right, preferred_element_type=jnp.float32)
+
+    @pl.when(step == pl.num_programs(0) - 1)
     def _():
-        density[...] = total[...].astype(jnp.bfloat16)
-
-
-def pairs(ints, floats, own, before, far, e_vir):
+        pair_sum = column[...] + row[...]
+        total = jnp.zeros(density.shape, jnp.float32)
+        for slot in range(2):
+            for rnd in range(2):
+                gap = pair_sum - floats[0, slot] - floats[1 + rnd, ints[slot, rnd]]
+                kept = ints[slot, 2 + rnd].astype(jnp.float32)
+                amp = (kept * meet[slot, rnd] / gap).astype(jnp.bfloat16)
+                amps[slot, rnd] = amp
+                total = total + lax.dot_general(
+                    amp, amp, (((1,), (1,)), ((), ())), preferred_element_type=jnp.float32
+                )
+        density[...] = total.astype(jnp.bfloat16)
+
+
+def finish(ids, ints, floats, metric, own, before, far, b2s, b2o, a2s, a2o, e_vir, tile=512):
     _, naux, nvir = own.shape
-    whole = pl.BlockSpec((2, naux, nvir), lambda s: (0, 0, 0))
     smem = pl.BlockSpec(memory_space=pltpu.SMEM)
+    sums = pl.BlockSpec((2, tile, nvir), lambda m, ids: (0, m, 0))
+    piece = pl.BlockSpec((1, 2, ROWS, nvir), lambda m, ids: (0, 0, 0, 0))
+    columns = [pl.BlockSpec((tile, ROWS), lambda m, ids, k=k: (m, ids[k])) for k in range(3)]
+    full = jax.ShapeDtypeStruct((2, naux, nvir), jnp.bfloat16)
     return pl.pallas_call(
-        pair_kernel,
+        finish_kernel,
         out_shape=(
             jax.ShapeDtypeStruct((2, 2, nvir, nvir), jnp.bfloat16),
             jax.ShapeDtypeStruct((nvir, nvir), jnp.bfloat16),
-        ),
-        grid=(2,),
-        in_specs=[
-            smem,
-            smem,
-            pl.BlockSpec((1, naux, nvir), lambda s: (s, 0, 0)),
-            whole,
-            whole,
-            pl.BlockSpec((1, nvir), lambda s: (0, 0)),
-            pl.BlockSpec((nvir, 1), lambda s: (0, 0)),
-        ],
-        out_specs=(
-            pl.BlockSpec((1, 2, nvir, nvir), lambda s: (s, 0, 0, 0)),
-            pl.BlockSpec((nvir, nvir), lambda s: (0, 0)),
-        ),
-        scratch_shapes=[pltpu.VMEM((nvir, nvir), jnp.float32)],
+            full,
+            full,
+        ),
+        grid_spec=pltpu.PrefetchScalarGridSpec(
+            num_scalar_prefetch=1,
+            grid=(naux // tile,),
+            in_specs=[smem, smem, *columns, sums, sums, sums, piece, piece, piece, piece]
+            + [
+                pl.BlockSpec((1, nvir), lambda m, ids: (0, 0)),
+                pl.BlockSpec((nvir, 1), lambda m, ids: (0, 0)),
+            ],
+            out_specs=(
+                pl.BlockSpec((2, 2, nvir, nvir), lambda m, ids: (0, 0, 0, 0)),
+                pl.BlockSpec((nvir, nvir), lambda m, ids: (0, 0)),
+                sums,
+                sums,
+            ),
+            scratch_shapes=[pltpu.VMEM((2, 2, nvir, nvir), jnp.float32)],
+        ),
         compiler_params=pltpu.CompilerParams(vmem_limit_bytes=VMEM),
         cost_estimate=pl.CostEstimate(
-            flops=8 * naux * nvir * nvir + 8 * nvir**3,
-            bytes_accessed=12 * naux * nvir,
+            flops=16 * naux * ROWS * nvir + 8 * naux * nvir * nvir + 8 * nvir**3,
+            bytes_accessed=32 * naux * nvir,
             transcendentals=0,
         ),
-        name="pairs",
-    )(ints, floats, own, before, far, e_vir[None, :], e_vir[:, None])
-
-
-def gradient_kernel(ints, amps, before, far, out):
+        name="finish",
+    )(
+        ids,
+        ints,
+        floats,
+        metric,
+        metric,
+        metric,
+        own,
+        before,
+        far,
+        b2s,
+        b2o,
+        a2s,
+        a2o,
+        e_vir[None, :],
+        e_vir[:, None],
+    )
+
+
+def gradient_kernel(ints, amps, before, far, *rest):
+    out = rest[-1]
     for slot in range(2):
         total = None
         for rnd, rights in enumerate((before, far)):
@@ -166,26 +233,31 @@
         out[:, slot, :] = total.astype(jnp.bfloat16)
 
 
-def gradient_of(ints, amps, before, far, tile=256):
+def gradient_of(ints, amps, before, far, upper=None, tile=256):
     _, naux, nvir = before.shape
-    rows = pl.BlockSpec((2, tile, nvir), lambda m: (0, m, 0))
+    steps = naux // tile // 2
+    first = 0 if upper is None else steps
+    rows = pl.BlockSpec((2, tile, nvir), lambda m: (0, m + first, 0))
+    rest = () if upper is None else (upper,)
     return pl.pallas_call(
         gradient_kernel,
         out_shape=jax.ShapeDtypeStruct((naux, 2, nvir), jnp.bfloat16),
-        grid=(naux // tile,),
+        grid=(steps,),
         in_specs=[
             pl.BlockSpec(memory_space=pltpu.SMEM),
             pl.BlockSpec((2, 2, nvir, nvir), lambda m: (0, 0, 0, 0)),
             rows,
             rows,
-        ],
-        out_specs=pl.BlockSpec((tile, 2, nvir), lambda m: (m, 0, 0)),
+        ]
+        + [pl.BlockSpec(memory_space=pl.ANY)] * len(rest),
+        out_specs=pl.BlockSpec((tile, 2, nvir), lambda m: (m + first, 0, 0)),
+        input_output_aliases={4: 0} if rest else {},
         compiler_params=pltpu.CompilerParams(vmem_limit_bytes=VMEM),
         cost_estimate=pl.CostEstimate(
-            flops=8 * naux * nvir * nvir, bytes_accessed=12 * naux * nvir, transcendentals=0
+            flops=4 * naux * nvir * nvir, bytes_accessed=6 * naux * nvir, transcendentals=0
         ),
         name="gradient",
-    )(ints, amps, before, far)
+    )(ints, amps, before, far, *rest)
 
 
 def summed_at_owner(array):
@@ -227,8 +299,16 @@
     a0o = send(other0, other_hop)
     y1 = send(jnp.concatenate(for_row(1)), along_y(1))
     y3 = send(jnp.concatenate(for_row(3)), along_y(3))
-    y1, y3, a0s, a0o, third = lax.optimization_barrier(
-        (y1, y3, a0s, a0o, jnp.concatenate(for_row(2)))
+    y1, y3, a0s, a0o, third, here0, below0 = lax.optimization_barrier(
+        (
+            y1,
+            y3,
+            a0s,
+            a0o,
+            jnp.concatenate(for_row(2)),
+            block((y * 2 + 7) % 8),
+            block((y * 2 + 5) % 8),
+        )
     )
     crosses = (device & 63) == 63
 
@@ -242,7 +322,9 @@
     half = send(third, along_y(3))
     b0s = send(a0o, same_hop)
     b0o = onward(same0, a0s)
-    r1 = send(jnp.concatenate([other0, other1]), next_row)
+    r1 = send(jnp.concatenate([other0, y1[1:]]), next_row)
+    near0 = send(jnp.where(x_hi == 0, here0, y3[1:]), to_row(0))
+    near3 = send(below0, to_row(3), (), lambda l: l & 1 == 0)
     a1s, a1o, half, b0s, b0o = lax.optimization_barrier((a1s, a1o, half, b0s, b0o))
     y2 = send(half, along_y(3))
     b1s = send(a1o, same_hop)
@@ -253,7 +335,9 @@
         [(a0s, 0, 0), (a1s, 0, 1), (a1s, 1, 2), (a0o, 0, 4), (a1o, 0, 5), (a1o, 1, 6)],
         dtype=wide,
     )
-    y2, b1s, b1o, r1, far = lax.optimization_barrier((y2, b1s, b1o, r1, far))
+    y2, b1s, b1o, r1, near0, near3, far = lax.optimization_barrier(
+        (y2, b1s, b1o, r1, near0, near3, far)
+    )
     a2s = send(y2[:1], same_hop)
     a2o = send(y2[1:], other_hop)
     own = transform(
@@ -263,28 +347,37 @@
         dtype=wide,
     )
     a2s, a2o, own = lax.optimization_barrier((a2s, a2o, own))
-    r2 = send(y2[1:], next_row)
+    near2 = jnp.where(x_hi == 0, near3, y2[1:])
     b2s = send(a2o, same_hop)
     b2o = onward(y2[:1], a2s)
 
     before = transform(
         metric,
         before_ids,
-        [(r1, 0, 0), (r1, 1, 1), (r1, 2, 2), (b0o, 0, 4), (b1o, 0, 5), (b1o, 1, 6)],
+        [
+            (r1, 0, 0),
+            (r1, 1, 1),
+            (near0, 0, 2),
+            (near2, 0, 3),
+            (b0o, 0, 4),
+            (b1o, 0, 5),
+            (b1o, 1, 6),
+        ],
         dtype=wide,
     )
-    far = transform(metric, own_ids, [(a2s, 0, 3), (a2o, 0, 7)], far)
-    own = transform(metric, own_ids, [(b2s, 0, 7)], own)
-    before = transform(metric, before_ids, [(r2, 0, 3), (b2o, 0, 7)], before)
 
     ints = jnp.concatenate([partner, screen], axis=1).astype(jnp.int32)
     owners = jnp.stack([device, (device - 1) % 128, (device - 64) % 128])
     floats = e_occ[owners[:, None] * 2 + jnp.arange(2)[None, :]]
-    amps, density = pairs(ints, floats, own, before, far, e_vir)
+    ids = jnp.stack([own_ids[3], own_ids[7], before_ids[7]])
+    amps, density, before, far = finish(
+        ids, ints, floats, metric, own, before, far, b2s, b2o, a2s, a2o, e_vir
+    )
     gradient = gradient_of(ints, amps, before, far)
-    rows = summed_at_owner(density)
-    total = summed_for_everyone(rows.astype(jnp.bfloat16))
-    return gradient, total / NOCC
+    rows = summed_at_owner(density).astype(jnp.bfloat16)
+    rows, amps = lax.optimization_barrier((rows, amps))
+    gradient = gradient_of(ints, amps, before, far, gradient)
+    return gradient, summed_for_everyone(rows) / NOCC
 
 
 def solution(mesh):

time: 243 us -> 234 us (0.963)
  Pallas kernels: 86.1 us -> 74 us
  waiting for transfers between devices: 56.2 us -> 46.5 us
  starting transfers between devices: 50.1 us -> 56.6 us
  other arithmetic: 15.7 us -> 20.2 us
    pallas_call x6 -> x3, Pallas kernels: 62.7 us -> 39.5 us  [transform(): pl.pallas_call(lambda *refs: transform_kernel(count, *refs), out_shape=ja...]
    ppermute x18 -> x19, starting transfers between devices: 36.9 us -> 49.6 us  [send(): lax.ppermute(array, AXES, [(l, to(l)) for l in range(128) if only(l)])]
    ppermute x18 -> x19, waiting for transfers between devices: 56.2 us -> 46.5 us  [send(): lax.ppermute(array, AXES, [(l, to(l)) for l in range(128) if only(l)])]
    pallas_call x1, Pallas kernels: 11.9 us -> 20.8 us  [finish(): pl.pallas_call(finish_kernel, out_shape=(jax.ShapeDtypeStruct((2, 2, nvir...]
    all_to_all x1, starting transfers between devices: 13.2 us -> 6.96 us  [summed_for_everyone(): arrived = lax.all_to_all(copies, 'aux', 0, 0, tiled=True)]
    another operation x0 -> x1, other arithmetic: none -> 2.56 us  [on_device(): ids = jnp.stack([own_ids[3], own_ids[7], before_ids[7]])]
    pallas_call x1 -> x2, Pallas kernels: 11.5 us -> 13.7 us  [gradient_of(): pl.pallas_call(gradient_kernel, out_shape=jax.ShapeDtypeStruct((naux, 2,...]
  transfers between devices with their start and end apart: 19 -> 20, of which waited for: 8 -> 5; matrix products, arithmetic and copies ran while one was open for 7% -> 9% of each run, Pallas kernels for 27% -> 23%
where the time goes in v4:
time: 234 us; the launch traced here: 233 us
  Pallas kernels  74 us (32%)
  starting transfers between devices  56.6 us (24%)
  waiting for transfers between devices  46.5 us (20%)
  other arithmetic  20.2 us (9%)
  local copies, waits for them, and re-layouts  18.6 us (8%)
  blocking collectives  16 us (7%)
    ppermute x19, starting transfers between devices, send(): lax.ppermute(array, AXES, [(l, to(l)) for l in range(128) if only(l)])  49.6 us
    ppermute x19, waiting for transfers between devices, send(): lax.ppermute(array, AXES, [(l, to(l)) for l in range(128) if only(l)])  46.5 us
    pallas_call x3, Pallas kernels, transform(): pl.pallas_call(lambda *refs: transform_kernel(count, *refs), out_shape=ja...  39.5 us
    pallas_call x1, Pallas kernels, finish(): pl.pallas_call(finish_kernel, out_shape=(jax.ShapeDtypeStruct((2, 2, nvir...  20.8 us
    all_to_all x1, blocking collectives, summed_at_owner(): lax.all_to_all(pieces, 'occ', split_axis=0, concat_axis=0, tiled=True)  16 us
    pallas_call x2, Pallas kernels, gradient_of(): pl.pallas_call(gradient_kernel, out_shape=jax.ShapeDtypeStruct((naux, 2,...  13.7 us
    all_to_all x1, starting transfers between devices, summed_for_everyone(): arrived = lax.all_to_all(copies, 'aux', 0, 0, tiled=True)  6.96 us
    transpose x1, local copies, waits for them, and re-layouts, on_device(): by_owner = jnp.transpose(integrals, (1, 0, 2)).reshape(8, 2, ROWS, nvir)  6.54 us
  transfers between devices with their start and end apart: 20, of which 5 were waited for; matrix products, arithmetic and copies ran while one was open for 9% of the time, Pallas kernels for 23%

profile of v4, /device:TPU:4, one launch (start us, length us, event | category | flops | bytes accessed | tf_op | source)
XLA Modules:
  0.0 232.9 jit_solution(5616645417600634585)
XLA Ops:
  0.8 6.5 %copy.13 = bf16[16,256,512]{2,1,0:T(8,128)(2,1)} copy(bf16[16,256,512]{2,0,1:T(8,128)(2,1)} %bitcast.11) | data formatting | bytes 8388608 | tf_op jit(solution)/shard_map/transpose | solution.py:281
  7.3 4.1 %constant_dynamic-slice_fusion = (bf16[1,2,256,512]{3,2,1,0:T(8,128)(2,1)}, bf16[1,2,256,512]{3,2,1,0:T(8,128)(2,1)}, bf16[1,2,256,512]{3,2,1,0:T(8,128)(2,1)}, ...) fusion(bf16[8,2,256,512]{3,2,1,0:T(8,128)(2,1)} %bitcast.10, ...), kind=kLoop, calls=%fused_computation.16 | loop fusion | bytes 10485800 | tf_op jit(solution)/shard_map/jit(dynamic_index_in_dim)/dynamic_slice | solution.py:284
  12.6 1.6 collective-permute-start
  15.3 1.7 collective-permute-start.1
  18.5 2.4 %pad_maximum_fusion.2 = bf16[2,2,256,512]{3,2,1,0:T(8,128)(2,1)} fusion(bf16[1,2,256,512]{3,2,1,0:T(8,128)(2,1)} %get-tuple-element.63, bf16[1,2,256,512]{3,2,1,0:T(8,128)(2,1)} %get-tuple-element.64), kind=kLoop, calls=%fused_computation.3 | loop fusion | flops 524288 | bytes 2097152 | tf_op jit(solution)/shard_map/concatenate | solution.py:308
  20.9 9.5 %collective-permute-done.3.refs_10_ = bf16[1,2,256,512]{3,2,1,0:T(8,128)(2,1)} collective-permute-done((bf16[1,2,256,512]{3,2,1,0:T(8,128)(2,1)}, bf16[1,2,256,512]{3,2,1,0:T(8,128)(2,1)}, u32[]{:S(2)}, u32[]{:S(2)}) %collective-permute-start.3) | collective-permute-done | bytes 524320 | tf_op jit(solution)/shard_map/ppermute | solution.py:55
  30.4 8.6 %collective-permute-done.refs_9_ = bf16[2,2,256,512]{3,2,1,0:T(8,128)(2,1)S(1)} collective-permute-done((bf16[2,2,256,512]{3,2,1,0:T(8,128)(2,1)}, bf16[2,2,256,512]{3,2,1,0:T(8,128)(2,1)S(1)}, u32[]{:S(2)}, u32[]{:S(2)}) %collective-permute-start) | collective-permute-done | bytes 1048608 | tf_op jit(solution)/shard_map/ppermute | solution.py:55
  41.2 3.0 %collective-permute-start.6 = (bf16[2,2,256,512]{3,2,1,0:T(8,128)(2,1)}, bf16[2,2,256,512]{3,2,1,0:T(8,128)(2,1)}, u32[]{:S(2)}, u32[]{:S(2)}) collective-permute-start(bf16[2,2,256,512]{3,2,1,0:T(8,128)(2,1)} %pad_maximum_fusion.2), channel_id=1, source_target_pairs={{0,6},{1,7},{2,0},{3,1},{4,2},{5,3},{6,4},{7,5},{8,14},{9,15},{10,... | collective-permute-start | bytes 3145736 | tf_op jit(solution)/shard_map/ppermute | solution.py:55
  44.2 2.1 broadcast_select_fusion.2
  46.3 2.5 %pad_maximum_fusion.5 = (bf16[2,2,256,512]{3,2,1,0:T(8,128)(2,1)}, bf16[2,2,256,512]{3,2,1,0:T(8,128)(2,1)}) fusion(bf16[1,2,256,512]{3,2,1,0:T(8,128)(2,1)S(1)} %get-tuple-element.78, bf16[1,2,256,512]{3,2,1,0:T(8,128)(2,1)} %get-tuple-element.65, bf16[1,2,256,512]{3,2,1,0:T(8,128)(2,1)S(1)} %get-tuple-element.76), kind=kLoop, calls=%fused_computation.6 | loop fusion | flops 1048576 | bytes 3670016 | tf_op jit(solution)/shard_map/concatenate | solution.py:325
  58.3 25.5 %collective-permute-done.8.refs_12_ = bf16[1,2,256,512]{3,2,1,0:T(8,128)(2,1)S(1)} collective-permute-done((bf16[1,2,256,512]{3,2,1,0:T(8,128)(2,1)}, bf16[1,2,256,512]{3,2,1,0:T(8,128)(2,1)S(1)}, u32[]{:S(2)}, u32[]{:S(2)}) %collective-permute-start.8) | collective-permute-done | bytes 524320 | tf_op jit(solution)/shard_map/ppermute | solution.py:55
  83.8 1.5 collective-permute-start.14
  85.3 1.9 collective-permute-start.12
  87.2 1.3 broadcast_select_fusion
  88.9 3.7 %collective-permute-start.11 = (bf16[2,2,256,512]{3,2,1,0:T(8,128)(2,1)}, bf16[2,2,256,512]{3,2,1,0:T(8,128)(2,1)}, u32[]{:S(2)}, u32[]{:S(2)}) collective-permute-start(bf16[2,2,256,512]{3,2,1,0:T(8,128)(2,1)} %broadcast_select_fusion), channel_id=1, source_target_pairs={{0,65},{1,66},{2,67},{3,68},{4,69},{5,70},{6,71},{7,72},{8,73},{9,... | collective-permute-start | bytes 3145736 | tf_op jit(solution)/shard_map/ppermute | solution.py:55
  92.6 2.4 %collective-permute-start.10 = (bf16[2,2,256,512]{3,2,1,0:T(8,128)(2,1)}, bf16[2,2,256,512]{3,2,1,0:T(8,128)(2,1)}, u32[]{:S(2)}, u32[]{:S(2)}) collective-permute-start(bf16[2,2,256,512]{3,2,1,0:T(8,128)(2,1)} %collective-permute-done.5.refs_11_.refs_12_), channel_id=1, source_target_pairs={{0,64},{1,65},{2,66},{3,67},{4,68},{5,69},{6,70},{7,71},{8,72},{9,... | collective-permute-start | bytes 3145736 | tf_op jit(solution)/shard_map/ppermute | solution.py:55
  96.1 2.6 %pad_add_fusion.1.ids = s32[3]{0:T(128)} fusion(s32[1]{0:T(128)} %slice.33, s32[1]{0:T(128)} %slice.32, s32[1]{0:T(128)} %slice.31), kind=kLoop, calls=%fused_computation.36 | loop fusion | flops 6 | bytes 24 | tf_op jit(solution)/shard_map/stack | solution.py:372
  99.3 5.3 %collective-permute-start.13 = (bf16[1,2,256,512]{3,2,1,0:T(8,128)(2,1)}, bf16[1,2,256,512]{3,2,1,0:T(8,128)(2,1)}, u32[]{:S(2)}, u32[]{:S(2)}) collective-permute-start(bf16[1,2,256,512]{3,2,1,0:T(8,128)(2,1)} %get-tuple-element.75), channel_id=1, source_target_pairs={{0,8},{1,1},{2,2},{3,3},{4,4},{5,5},{6,6},{7,7},{8,16},{9,9},{10,1... | collective-permute-start | bytes 1572872 | tf_op jit(solution)/shard_map/ppermute | solution.py:55
  104.7 12.3 %transform.3.far_sum = f32[2,2048,512]{2,1,0:T(8,128)} custom-call(s32[8]{0:T(128)} %pad_add_fusion.2.refs_0_, bf16[2048,2048]{1,0:T(8,128)(2,1)} %m_late.1, bf16[2048,2048]{1,0:T(8,128)(2,1)} %m_late.1, bf16[2048,2048]{1,0:T(8,128)(2,1)} %m_late.1, bf16[2048,2048]{1,0:T(8,128)(2,1)} %m_late.1, bf16[2048,2048]{1,0:T(8,128)(2,1)} %m_late.1, ...), custom_call_target="tpu_custom_call" | custom-call | flops 6442450944 | bytes 17825792 | tf_op jit(solution)/shard_map/transform/pallas_call | solution.py:84
  117.1 1.7 collective-permute-done.10.refs_13_.refs_14_
  119.8 17.4 %collective-permute-start.16 = (bf16[1,2,256,512]{3,2,1,0:T(8,128)(2,1)}, bf16[1,2,256,512]{3,2,1,0:T(8,128)(2,1)S(1)}, u32[]{:S(2)}, u32[]{:S(2)}) collective-permute-start(bf16[1,2,256,512]{3,2,1,0:T(8,128)(2,1)} %get-tuple-element.73), channel_id=1, source_target_pairs={{0,65},{1,64},{2,67},{3,66},{4,69},{5,68},{6,71},{7,70},{8,73},{9,... | collective-permute-start | bytes 1572872 | tf_op jit(solution)/shard_map/ppermute | solution.py:55
  137.2 2.3 collective-permute-start.15
  139.5 13.6 %transform.4.own_sum = f32[2,2048,512]{2,1,0:T(8,128)} custom-call(s32[8]{0:T(128)} %pad_add_fusion.2.refs_0_, bf16[2048,2048]{1,0:T(8,128)(2,1)} %m_late.1, bf16[2048,2048]{1,0:T(8,128)(2,1)} %m_late.1, bf16[2048,2048]{1,0:T(8,128)(2,1)} %m_late.1, bf16[2048,2048]{1,0:T(8,128)(2,1)} %m_late.1, bf16[2048,2048]{1,0:T(8,128)(2,1)} %m_late.1, ...), custom_call_target="tpu_custom_call" | custom-call | flops 7516192768 | bytes 19398656 | tf_op jit(solution)/shard_map/transform/pallas_call | solution.py:84
  153.1 2.5 %broadcast_select_fusion.3 = (bf16[1,2,256,512]{3,2,1,0:T(8,128)(2,1)S(1)}, bf16[1,2,256,512]{3,2,1,0:T(8,128)(2,1)}) fusion(bf16[1,2,256,512]{3,2,1,0:T(8,128)(2,1)S(1)} %collective-permute-done.15.a2s, pred[]{:T(512)S(6)} %eq.20, bf16[2,2,256,512]{3,2,1,0:T(8,128)(2,1)} %copy-done.3, bf16[1,2,256,512]{3,2,1,0:T(8,128)(2,1)} %collective-permute-done.14, ...), kind=kLoop, calls=%fused_computation.11 | loop fusion | flops 524288 | bytes 3145730 | tf_op jit(solution)/shard_map/jit(_where)/select_n | solution.py:316
  155.6 1.4 collective-permute-start.18
  157.0 2.4 %collective-permute-start.17 = (bf16[1,2,256,512]{3,2,1,0:T(8,128)(2,1)S(1)}, bf16[1,2,256,512]{3,2,1,0:T(8,128)(2,1)S(1)}, u32[]{:S(2)}, u32[]{:S(2)}) collective-permute-start(bf16[1,2,256,512]{3,2,1,0:T(8,128)(2,1)S(1)} %collective-permute-done.16.a2o), channel_id=1, source_target_pairs={{0,64},{1,65},{2,66},{3,67},{4,68},{5,69},{6,70},{7,71},{8,72},{9,... | collective-permute-start | bytes 1572872 | tf_op jit(solution)/shard_map/ppermute | solution.py:55
  159.3 13.6 %transform.5.before_sum = f32[2,2048,512]{2,1,0:T(8,128)} custom-call(s32[8]{0:T(128)} %pad_add_fusion.3.refs_0_, bf16[2048,2048]{1,0:T(8,128)(2,1)} %m_late.1, bf16[2048,2048]{1,0:T(8,128)(2,1)} %m_late.1, bf16[2048,2048]{1,0:T(8,128)(2,1)} %m_late.1, bf16[2048,2048]{1,0:T(8,128)(2,1)} %m_late.1, bf16[2048,2048]{1,0:T(8,128)(2,1)} %m_late.1, ...), custom_call_target="tpu_custom_call" | custom-call | flops 7516192768 | bytes 19398656 | tf_op jit(solution)/shard_map/transform/pallas_call | solution.py:84
  174.0 20.8 %finish.1 = (bf16[2,2,512,512]{3,2,1,0:T(8,128)(2,1)}, bf16[512,512]{1,0:T(8,128)(2,1)}, bf16[2,2048,512]{2,1,0:T(8,128)(2,1)}, bf16[2,2048,512]{2,1,0:T(8,128)(2,1)}) custom-call(s32[3]{0:T(128)} %pad_add_fusion.1.ids, s32[2,4]{1,0:T(2,128)} %pad_add_fusion.ints, f32[3,2]{1,0:T(4,128)} %reshape.79.floats, bf16[2048,2048]{1,0:T(8,128)(2,1)} %m_late.1, ...), custom_call_target="tpu_custom_call" | custom-call | flops 9663676416 | bytes 33554432 | tf_op jit(solution)/shard_map/finish/pallas_call | solution.py:171
  194.8 16.0 %all_to_all.10 = bf16[16,32,512]{2,1,0:T(8,128)(2,1)S(1)} all-to-all(bf16[16,32,512]{2,1,0:T(8,128)(2,1)} %bitcast.12), channel_id=1, replica_groups=mesh['occ'=16,'aux'=8] {'occ'}, dimensions={0} | all-to-all | bytes 1048576 | tf_op jit(solution)/shard_map/all_to_all | solution.py:265
  211.6 7.0 %all-to-all-start.1 = ((bf16[8,32,512]{2,1,0:T(8,128)(2,1)}), bf16[8,32,512]{2,1,0:T(8,128)(2,1)S(1)}, u32[]{:S(2)}, u32[]{:S(2)}) async-start(bf16[8,32,512]{2,1,0:T(8,128)(2,1)} %broadcast_in_dim.8), calls=%async_computation.1 | async-start | bytes 524288 | tf_op jit(solution)/shard_map/all_to_all | solution.py:271
  218.6 6.8 %gradient.2.rest_0_ = bf16[2048,2,512]{2,1,0:T(2,128)(2,1)} custom-call(s32[2,4]{1,0:T(2,128)} %pad_add_fusion.ints, bf16[2,2,512,512]{3,2,1,0:T(8,128)(2,1)} %get-tuple-element.54.amps, bf16[2,2048,512]{2,1,0:T(8,128)(2,1)} %get-tuple-element.55.before, bf16[2,2048,512]{2,1,0:T(8,128)(2,1)} %get-tuple-element.56.far), custom_call_target="tpu_custom_call" | custom-call | flops 2147483648 | bytes 6291456 | tf_op jit(solution)/shard_map/gradient/pallas_call | solution.py:242
  225.4 6.8 %gradient.3 = bf16[2048,2,512]{2,1,0:T(2,128)(2,1)} custom-call(s32[2,4]{1,0:T(2,128)} %pad_add_fusion.ints, bf16[2,2,512,512]{3,2,1,0:T(8,128)(2,1)} %get-tuple-element.54.amps, bf16[2,2048,512]{2,1,0:T(8,128)(2,1)} %get-tuple-element.55.before, bf16[2,2048,512]{2,1,0:T(8,128)(2,1)} %get-tuple-element.56.far, ...), custom_call_target="tpu_custom_call", output_to_operand_aliasing={{}: (4, {})} | custom-call | flops 2147483648 | bytes 6291456 | tf_op jit(solution)/shard_map/gradient/pallas_call | solution.py:242
  (87 shorter events, 21.0 us)
Async XLA Ops:
  0.6 55.5 %copy-start = (f32[256]{0:T(256)S(1)}, f32[256]{0:T(256)}, u32[]{:S(2)}) copy-start(f32[256]{0:T(256)} %param.9) | copy-start | bytes 3076
  11.5 40.1 %copy-start.4 = (bf16[1,2,256,512]{3,2,1,0:T(8,128)(2,1)}, bf16[1,2,256,512]{3,2,1,0:T(8,128)(2,1)S(1)}, u32[]{:S(2)}) copy-start(bf16[1,2,256,512]{3,2,1,0:T(8,128)(2,1)S(1)} %get-tuple-element.66.refs_8_) | copy-start | bytes 1572868
  12.6 26.4 %collective-permute-start = (bf16[2,2,256,512]{3,2,1,0:T(8,128)(2,1)}, bf16[2,2,256,512]{3,2,1,0:T(8,128)(2,1)S(1)}, u32[]{:S(2)}, u32[]{:S(2)}) collective-permute-start(bf16[2,2,256,512]{3,2,1,0:T(8,128)(2,1)} %pad_maximum_fusion), channel_id=1, source_target_pairs={{0,2},{1,3},{2,4},{3,5},{4,6},{5,7},{6,0},{7,1},{8,10},{9,11},{10,... | collective-permute-start | bytes 3145736 | tf_op jit(solution)/shard_map/ppermute | solution.py:55
  15.3 24.8 %collective-permute-start.1 = (bf16[2,2,256,512]{3,2,1,0:T(8,128)(2,1)}, bf16[2,2,256,512]{3,2,1,0:T(8,128)(2,1)S(1)}, u32[]{:S(2)}, u32[]{:S(2)}) collective-permute-start(bf16[2,2,256,512]{3,2,1,0:T(8,128)(2,1)} %pad_maximum_fusion.1), channel_id=1, source_target_pairs={{0,6},{1,7},{2,0},{3,1},{4,2},{5,3},{6,4},{7,5},{8,14},{9,15},{10,... | collective-permute-start | bytes 3145736 | tf_op jit(solution)/shard_map/ppermute | solution.py:55
  16.9 13.5 %collective-permute-start.3 = (bf16[1,2,256,512]{3,2,1,0:T(8,128)(2,1)}, bf16[1,2,256,512]{3,2,1,0:T(8,128)(2,1)}, u32[]{:S(2)}, u32[]{:S(2)}) collective-permute-start(bf16[1,2,256,512]{3,2,1,0:T(8,128)(2,1)} %get-tuple-element.65), channel_id=1, source_target_pairs={{0,65},{1,64},{2,67},{3,66},{4,69},{5,68},{6,71},{7,70},{8,73},{9,... | collective-permute-start | bytes 1572872 | tf_op jit(solution)/shard_map/ppermute | solution.py:55
  17.5 13.0 %collective-permute-start.2 = (bf16[1,2,256,512]{3,2,1,0:T(8,128)(2,1)S(1)}, bf16[1,2,256,512]{3,2,1,0:T(8,128)(2,1)S(1)}, u32[]{:S(2)}, u32[]{:S(2)}) collective-permute-start(bf16[1,2,256,512]{3,2,1,0:T(8,128)(2,1)S(1)} %get-tuple-element.66.refs_8_), channel_id=1, source_target_pairs={{0,64},{1,65},{2,66},{3,67},{4,68},{5,69},{6,70},{7,71},{8,72},{9,... | collective-permute-start | bytes 1572872 | tf_op jit(solution)/shard_map/ppermute | solution.py:55
  18.5 25.7 %copy-start.10 = (bf16[1,2,256,512]{3,2,1,0:T(8,128)(2,1)S(1)}, bf16[1,2,256,512]{3,2,1,0:T(8,128)(2,1)}, u32[]{:S(2)}) copy-start(bf16[1,2,256,512]{3,2,1,0:T(8,128)(2,1)} %get-tuple-element.38) | copy-start | bytes 1572868
  30.4 54.9 %copy-start.8 = (bf16[1,2,256,512]{3,2,1,0:T(8,128)(2,1)}, bf16[1,2,256,512]{3,2,1,0:T(8,128)(2,1)S(1)}, u32[]{:S(2)}) copy-start(bf16[1,2,256,512]{3,2,1,0:T(8,128)(2,1)S(1)} %collective-permute-done.2.refs_7_) | copy-start | bytes 1572868
  41.2 46.0 %collective-permute-start.6 = (bf16[2,2,256,512]{3,2,1,0:T(8,128)(2,1)}, bf16[2,2,256,512]{3,2,1,0:T(8,128)(2,1)}, u32[]{:S(2)}, u32[]{:S(2)}) collective-permute-start(bf16[2,2,256,512]{3,2,1,0:T(8,128)(2,1)} %pad_maximum_fusion.2), channel_id=1, source_target_pairs={{0,6},{1,7},{2,0},{3,1},{4,2},{5,3},{6,4},{7,5},{8,14},{9,15},{10,... | collective-permute-start | bytes 3145736 | tf_op jit(solution)/shard_map/ppermute | solution.py:55
  48.9 38.3 %collective-permute-start.5 = (bf16[2,2,256,512]{3,2,1,0:T(8,128)(2,1)}, bf16[2,2,256,512]{3,2,1,0:T(8,128)(2,1)}, u32[]{:S(2)}, u32[]{:S(2)}) collective-permute-start(bf16[2,2,256,512]{3,2,1,0:T(8,128)(2,1)} %get-tuple-element.81), channel_id=1, source_target_pairs={{0,65},{1,64},{2,67},{3,66},{4,69},{5,68},{6,71},{7,70},{8,73},{9,... | collective-permute-start | bytes 3145736 | tf_op jit(solution)/shard_map/ppermute | solution.py:55
  49.4 49.3 %copy-start.16 = (s32[2,2]{1,0:T(2,128)S(1)}, s32[2,2]{1,0:T(2,128)}, u32[]{:S(2)}) copy-start(s32[2,2]{1,0:T(2,128)} %param.12) | copy-start | bytes 52
  49.4 49.3 %copy-start.17 = (s32[2,2]{1,0:T(2,128)S(1)}, s32[2,2]{1,0:T(2,128)}, u32[]{:S(2)}) copy-start(s32[2,2]{1,0:T(2,128)} %param.11) | copy-start | bytes 52
  50.4 36.7 %collective-permute-start.4 = (bf16[2,2,256,512]{3,2,1,0:T(8,128)(2,1)}, bf16[2,2,256,512]{3,2,1,0:T(8,128)(2,1)S(1)}, u32[]{:S(2)}, u32[]{:S(2)}) collective-permute-start(bf16[2,2,256,512]{3,2,1,0:T(8,128)(2,1)} %pad_maximum_fusion.3), channel_id=1, source_target_pairs={{0,64},{1,65},{2,66},{3,67},{4,68},{5,69},{6,70},{7,71},{8,72},{9,... | collective-permute-start | bytes 3145736 | tf_op jit(solution)/shard_map/ppermute | solution.py:55
  52.4 31.4 %collective-permute-start.8 = (bf16[1,2,256,512]{3,2,1,0:T(8,128)(2,1)}, bf16[1,2,256,512]{3,2,1,0:T(8,128)(2,1)S(1)}, u32[]{:S(2)}, u32[]{:S(2)}) collective-permute-start(bf16[1,2,256,512]{3,2,1,0:T(8,128)(2,1)} %broadcast_select_fusion.4), channel_id=1, source_target_pairs={{0,65},{1,66},{2,67},{3,68},{4,69},{5,70},{6,71},{7,72},{8,73},{9,... | collective-permute-start | bytes 1572872 | tf_op jit(solution)/shard_map/ppermute | solution.py:55
  53.1 32.2 %collective-permute-start.7 = (bf16[1,2,256,512]{3,2,1,0:T(8,128)(2,1)}, bf16[1,2,256,512]{3,2,1,0:T(8,128)(2,1)}, u32[]{:S(2)}, u32[]{:S(2)}) collective-permute-start(bf16[1,2,256,512]{3,2,1,0:T(8,128)(2,1)} %collective-permute-done.3.refs_10_), channel_id=1, source_target_pairs={{0,64},{1,65},{2,66},{3,67},{4,68},{5,69},{6,70},{7,71},{8,72},{9,... | collective-permute-start | bytes 1572872 | tf_op jit(solution)/shard_map/ppermute | solution.py:55
  83.8 33.2 %copy-start.11 = (bf16[1,2,256,512]{3,2,1,0:T(8,128)(2,1)}, bf16[1,2,256,512]{3,2,1,0:T(8,128)(2,1)S(1)}, u32[]{:S(2)}) copy-start(bf16[1,2,256,512]{3,2,1,0:T(8,128)(2,1)S(1)} %collective-permute-done.8.refs_12_) | copy-start | bytes 1572868
  83.8 15.5 %collective-permute-start.14 = (bf16[1,2,256,512]{3,2,1,0:T(8,128)(2,1)}, bf16[1,2,256,512]{3,2,1,0:T(8,128)(2,1)}, u32[]{:S(2)}, u32[]{:S(2)}) collective-permute-start(bf16[1,2,256,512]{3,2,1,0:T(8,128)(2,1)} %get-tuple-element.39), channel_id=1, source_target_pairs={{0,6},{2,8},{4,2},{6,4},{8,14},{10,16},{12,10},{14,12},{16,22},{18... | collective-permute-start | bytes 1572872 | tf_op jit(solution)/shard_map/ppermute | solution.py:55
  85.3 31.7 %collective-permute-start.12 = (bf16[2,2,256,512]{3,2,1,0:T(8,128)(2,1)}, bf16[2,2,256,512]{3,2,1,0:T(8,128)(2,1)S(1)}, u32[]{:S(2)}, u32[]{:S(2)}) collective-permute-start(bf16[2,2,256,512]{3,2,1,0:T(8,128)(2,1)} %get-tuple-element.80), channel_id=1, source_target_pairs={{0,2},{1,1},{2,4},{3,3},{4,6},{5,5},{6,8},{7,7},{8,10},{9,9},{10,1... | collective-permute-start | bytes 3145736 | tf_op jit(solution)/shard_map/ppermute | solution.py:55
  87.2 17.5 %copy-start.2 = (bf16[2,2,256,512]{3,2,1,0:T(8,128)(2,1)}, bf16[2,2,256,512]{3,2,1,0:T(8,128)(2,1)S(1)}, u32[]{:S(2)}) copy-start(bf16[2,2,256,512]{3,2,1,0:T(8,128)(2,1)S(1)} %collective-permute-done.4.refs_8_.refs_9_) | copy-start | bytes 3145732
  88.5 28.6 %collective-permute-start.9 = (bf16[2,2,256,512]{3,2,1,0:T(8,128)(2,1)}, bf16[2,2,256,512]{3,2,1,0:T(8,128)(2,1)S(1)}, u32[]{:S(2)}, u32[]{:S(2)}) collective-permute-start(bf16[2,2,256,512]{3,2,1,0:T(8,128)(2,1)} %collective-permute-done.6), channel_id=1, source_target_pairs={{0,6},{1,7},{2,0},{3,1},{4,2},{5,3},{6,4},{7,5},{8,14},{9,15},{10,... | collective-permute-start | bytes 3145736 | tf_op jit(solution)/shard_map/ppermute | solution.py:55
  88.9 28.1 %collective-permute-start.11 = (bf16[2,2,256,512]{3,2,1,0:T(8,128)(2,1)}, bf16[2,2,256,512]{3,2,1,0:T(8,128)(2,1)}, u32[]{:S(2)}, u32[]{:S(2)}) collective-permute-start(bf16[2,2,256,512]{3,2,1,0:T(8,128)(2,1)} %broadcast_select_fusion), channel_id=1, source_target_pairs={{0,65},{1,66},{2,67},{3,68},{4,69},{5,70},{6,71},{7,72},{8,73},{9,... | collective-permute-start | bytes 3145736 | tf_op jit(solution)/shard_map/ppermute | solution.py:55
  92.6 26.2 %collective-permute-start.10 = (bf16[2,2,256,512]{3,2,1,0:T(8,128)(2,1)}, bf16[2,2,256,512]{3,2,1,0:T(8,128)(2,1)}, u32[]{:S(2)}, u32[]{:S(2)}) collective-permute-start(bf16[2,2,256,512]{3,2,1,0:T(8,128)(2,1)} %collective-permute-done.5.refs_11_.refs_12_), channel_id=1, source_target_pairs={{0,64},{1,65},{2,66},{3,67},{4,68},{5,69},{6,70},{7,71},{8,72},{9,... | collective-permute-start | bytes 3145736 | tf_op jit(solution)/shard_map/ppermute | solution.py:55
  99.3 17.7 %collective-permute-start.13 = (bf16[1,2,256,512]{3,2,1,0:T(8,128)(2,1)}, bf16[1,2,256,512]{3,2,1,0:T(8,128)(2,1)}, u32[]{:S(2)}, u32[]{:S(2)}) collective-permute-start(bf16[1,2,256,512]{3,2,1,0:T(8,128)(2,1)} %get-tuple-element.75), channel_id=1, source_target_pairs={{0,8},{1,1},{2,2},{3,3},{4,4},{5,5},{6,6},{7,7},{8,16},{9,9},{10,1... | collective-permute-start | bytes 1572872 | tf_op jit(solution)/shard_map/ppermute | solution.py:55
  117.0 36.0 %copy-start.5 = (bf16[2,2,256,512]{3,2,1,0:T(8,128)(2,1)}, bf16[2,2,256,512]{3,2,1,0:T(8,128)(2,1)S(1)}, u32[]{:S(2)}) copy-start(bf16[2,2,256,512]{3,2,1,0:T(8,128)(2,1)S(1)} %collective-permute-done.12.refs_8_.refs_9_) | copy-start | bytes 3145732
  117.1 22.4 %copy-start.3 = (bf16[2,2,256,512]{3,2,1,0:T(8,128)(2,1)}, bf16[2,2,256,512]{3,2,1,0:T(8,128)(2,1)S(1)}, u32[]{:S(2)}) copy-start(bf16[2,2,256,512]{3,2,1,0:T(8,128)(2,1)S(1)} %collective-permute-done.9.refs_11_) | copy-start | bytes 3145732
  119.8 33.3 %collective-permute-start.16 = (bf16[1,2,256,512]{3,2,1,0:T(8,128)(2,1)}, bf16[1,2,256,512]{3,2,1,0:T(8,128)(2,1)S(1)}, u32[]{:S(2)}, u32[]{:S(2)}) collective-permute-start(bf16[1,2,256,512]{3,2,1,0:T(8,128)(2,1)} %get-tuple-element.73), channel_id=1, source_target_pairs={{0,65},{1,64},{2,67},{3,66},{4,69},{5,68},{6,71},{7,70},{8,73},{9,... | collective-permute-start | bytes 1572872 | tf_op jit(solution)/shard_map/ppermute | solution.py:55
  137.2 15.9 %collective-permute-start.15 = (bf16[1,2,256,512]{3,2,1,0:T(8,128)(2,1)S(1)}, bf16[1,2,256,512]{3,2,1,0:T(8,128)(2,1)S(1)}, u32[]{:S(2)}, u32[]{:S(2)}) collective-permute-start(bf16[1,2,256,512]{3,2,1,0:T(8,128)(2,1)S(1)} %get-tuple-element.74), channel_id=1, source_target_pairs={{0,64},{1,65},{2,66},{3,67},{4,68},{5,69},{6,70},{7,71},{8,72},{9,... | collective-permute-start | bytes 1572872 | tf_op jit(solution)/shard_map/ppermute | solution.py:55
  153.1 19.9 %copy-start.12 = (bf16[1,2,256,512]{3,2,1,0:T(8,128)(2,1)}, bf16[1,2,256,512]{3,2,1,0:T(8,128)(2,1)S(1)}, u32[]{:S(2)}) copy-start(bf16[1,2,256,512]{3,2,1,0:T(8,128)(2,1)S(1)} %collective-permute-done.16.a2o) | copy-start | bytes 1572868
  153.1 19.9 %copy-start.9 = (bf16[1,2,256,512]{3,2,1,0:T(8,128)(2,1)}, bf16[1,2,256,512]{3,2,1,0:T(8,128)(2,1)S(1)}, u32[]{:S(2)}) copy-start(bf16[1,2,256,512]{3,2,1,0:T(8,128)(2,1)S(1)} %collective-permute-done.15.a2s) | copy-start | bytes 1572868
  155.6 17.4 %collective-permute-start.18 = (bf16[1,2,256,512]{3,2,1,0:T(8,128)(2,1)S(1)}, bf16[1,2,256,512]{3,2,1,0:T(8,128)(2,1)S(1)}, u32[]{:S(2)}, u32[]{:S(2)}) collective-permute-start(bf16[1,2,256,512]{3,2,1,0:T(8,128)(2,1)S(1)} %get-tuple-element.71), channel_id=1, source_target_pairs={{0,65},{1,66},{2,67},{3,68},{4,69},{5,70},{6,71},{7,72},{8,73},{9,... | collective-permute-start | bytes 1572872 | tf_op jit(solution)/shard_map/ppermute | solution.py:55
  157.0 16.0 %collective-permute-start.17 = (bf16[1,2,256,512]{3,2,1,0:T(8,128)(2,1)S(1)}, bf16[1,2,256,512]{3,2,1,0:T(8,128)(2,1)S(1)}, u32[]{:S(2)}, u32[]{:S(2)}) collective-permute-start(bf16[1,2,256,512]{3,2,1,0:T(8,128)(2,1)S(1)} %collective-permute-done.16.a2o), channel_id=1, source_target_pairs={{0,64},{1,65},{2,66},{3,67},{4,68},{5,69},{6,70},{7,71},{8,72},{9,... | collective-permute-start | bytes 1572872 | tf_op jit(solution)/shard_map/ppermute | solution.py:55
  211.6 20.6 %all-to-all-start.1 = ((bf16[8,32,512]{2,1,0:T(8,128)(2,1)}), bf16[8,32,512]{2,1,0:T(8,128)(2,1)S(1)}, u32[]{:S(2)}, u32[]{:S(2)}) async-start(bf16[8,32,512]{2,1,0:T(8,128)(2,1)} %broadcast_in_dim.8), calls=%async_computation.1 | async-start | bytes 524288 | tf_op jit(solution)/shard_map/all_to_all | solution.py:271
  (7 other events, 40.6 us)
